TPU v7x, 128 devices: a whole 4x4x4 slice. The times are simulated.
128 devices in a mesh: elem: 128 (over y, x, z, core).
Axes of the slice: x: 4, y: 4, z: 4, core: 2. Of those that a mesh axis runs over, the one named last changes fastest.
Arguments:
- a_blocks: float32 [4096, 7, 4096], P('elem'), may hold values from -0.25 to 0.25
- p_blocks: float32 [4096, 2, 4096], P('elem'), may hold values from -1.2 to 1.2
- a_slot: int32 [4096, 7], P('elem'), may hold values from 0 to 285
- serve_rows: int32 [128, 127, 2], P('elem'), may hold values from 0 to 31
- row_count: int32 [128], P('elem'), may hold values from 8 to 32, as said below
- contrib_slot: int32 [4096, 28], P('elem'), may hold values from 0 to 511
- recv_tile: int32 [128, 128, 4], P('elem'), may hold values from 0 to 7
Outputs:
- coarse: float32 [1024, 4096], P('elem')
Inputs may be any that keep to these rules, and one draw needn't show every extreme that they name: `row_count`: rows of a device at or beyond its count are padding and contribute nothing; some device has exactly 32.
All inputs are finite; a program needn't handle non-finite values.
Results may differ from a plain program's by a relative error of at most 0.0003.
Values sent between devices are 32-bit elements; how exact they have to be, the bound alone decides.
A program may use at most 192 MiB of HBM per device.

v0:
```python
import jax
import jax.numpy as jnp
from jax import lax
from jax.sharding import PartitionSpec as P

B = 64
KA = 7
KP = 2
S = 2
CAP = 4
TO = 8


def body(a_blocks, p_blocks, a_slot, serve_rows, row_count, contrib_slot, recv_tile):
    count_dev = lax.axis_size("elem")
    myself = lax.axis_index("elem")
    rows = a_blocks.shape[0]
    count_near = count_dev - 1
    a_tiles = a_blocks.reshape(rows, KA, B, B)
    live = (jnp.arange(rows, dtype=jnp.int32) < row_count[0]).astype(jnp.float32)
    p_masked = p_blocks.reshape(rows, KP, B, B) * live[:, None, None, None]
    outgoing = p_blocks[serve_rows[0]]
    by_offset = jnp.concatenate([jnp.zeros((1, S, KP, B * B), jnp.float32), outgoing], axis=0)
    buffer = jnp.roll(by_offset, myself, axis=0)
    arrived = lax.all_to_all(buffer, "elem", split_axis=0, concat_axis=0, tiled=True)
    back_order = jnp.roll(arrived[::-1], myself + 1, axis=0)
    fetched = back_order[1:]
    extended = jnp.concatenate([p_blocks, fetched.reshape(count_near * S, KP, B * B)], axis=0)
    neigh = extended[a_slot].reshape(rows, KA, KP, B, B)
    product = jnp.einsum("ikxy,ikqyz->ikqxz", a_tiles, neigh, precision=lax.Precision.HIGHEST)
    part = jnp.einsum("ipyx,ikqyz->ipkqxz", p_masked, product, precision=lax.Precision.HIGHEST)
    slot_range = jnp.arange(count_dev * CAP, dtype=jnp.int32)
    slot_table = (slot_range[:, None] == contrib_slot.reshape(1, -1)).astype(jnp.float32)
    slots = jnp.dot(slot_table, part.reshape(-1, B * B), precision=lax.Precision.HIGHEST)
    slot_three = slots.reshape(count_dev, CAP, B * B)
    tile_buffer = jnp.roll(slot_three, myself, axis=0)
    tile_arrived = lax.all_to_all(tile_buffer, "elem", split_axis=0, concat_axis=0, tiled=True)
    gotten = jnp.roll(tile_arrived[::-1], myself + 1, axis=0)
    tile_range = jnp.arange(TO, dtype=jnp.int32)
    tile_table = (tile_range[:, None] == recv_tile[0].reshape(1, -1)).astype(jnp.float32)
    coarse = jnp.dot(
        tile_table, gotten.reshape(count_dev * CAP, B * B), precision=lax.Precision.HIGHEST
    )
    return coarse


def solution(mesh):
    in_specs = (
        P("elem", None, None),
        P("elem", None, None),
        P("elem", None),
        P("elem", None, None),
        P("elem"),
        P("elem", None),
        P("elem", None, None),
    )
    out_specs = P("elem", None)
    return jax.shard_map(body, mesh=mesh, in_specs=in_specs, out_specs=out_specs, check_vma=False)
```

profile of v0, /device:TPU:1, one launch (start us, length us, event | category | flops | bytes accessed | tf_op | source)
XLA Modules:
  0.0 521.2 jit_solution(2843255759208246293)
XLA Ops:
  1.0 15.9 %gather_fusion = f32[254,2,4096]{2,1,0:T(2,128)} fusion(f32[32,2,4096]{2,1,0:T(2,128)} %param.12, s32[1024]{0:T(1024)S(1)} %pad_clamp_fusion.1), kind=kCustom, calls=%fused_computation | custom fusion | bytes 16647160 | tf_op jit(solution)/shard_map/gather | solution.py:22
  16.9 5.5 %concatenate.12 = f32[128,2,2,4096]{3,2,1,0:T(2,128)S(1)} pad(f32[127,2,2,4096]{3,2,1,0:T(2,128)} %bitcast.35, f32[]{:T(128)} %constant.45.clone.1), padding=1_0x0_0x0_0x0_0 | pad | bytes 16711684 | tf_op jit(solution)/shard_map/concatenate | solution.py:23
  22.4 10.2 %fusion.7 = f32[128,2,2,4096]{3,2,1,0:T(2,128)} fusion(s32[]{:T(128)S(6)} %select_n.37, f32[128,2,2,4096]{3,2,1,0:T(2,128)S(1)} %concatenate.12), kind=kLoop, calls=%fused_computation.16 | loop fusion | flops 2097152 | bytes 16777220 | tf_op jit(solution)/shard_map/jit(_roll_dynamic)/concatenate | solution.py:24
  32.7 12.3 %all-to-all-start = ((f32[128,2,2,4096]{3,2,1,0:T(2,128)}), f32[128,2,2,4096]{3,2,1,0:T(2,128)}, u32[]{:S(2)}, u32[]{:S(2)}) async-start(f32[128,2,2,4096]{3,2,1,0:T(2,128)} %fusion.7), calls=%async_computation | async-start | bytes 16777216 | tf_op jit(solution)/shard_map/all_to_all | solution.py:25
  46.4 7.0 %reshape.75 = f32[32,7,64,64]{3,2,0,1:T(8,128)} reshape(f32[32,7,4096]{2,0,1:T(8,128)} %param.11) | data formatting | bytes 7340032 | tf_op jit(solution)/shard_map/reshape | solution.py:19
  54.2 91.8 %all-to-all-done = f32[128,2,2,4096]{3,2,1,0:T(2,128)} async-done(((f32[128,2,2,4096]{3,2,1,0:T(2,128)}), f32[128,2,2,4096]{3,2,1,0:T(2,128)}, u32[]{:S(2)}, u32[]{:S(2)}) %all-to-all-start) | async-done | bytes 8388640 | tf_op jit(solution)/shard_map/all_to_all | solution.py:25
  146.0 9.1 %rev.6 = f32[128,2,2,4096]{3,2,1,0:T(2,128)} reverse(f32[128,2,2,4096]{3,2,1,0:T(2,128)} %all-to-all-done), dimensions={0} | reverse | bytes 16777216 | tf_op jit(solution)/shard_map/rev | solution.py:26
  155.1 19.7 %fusion.8 = f32[127,2,2,4096]{3,2,1,0:T(2,128)S(1)} fusion(s32[]{:T(128)S(6)} %add.61, f32[128,2,2,4096]{3,2,1,0:T(2,128)} %rev.6), kind=kLoop, calls=%fused_computation.17 | loop fusion | flops 2080768 | bytes 16711684 | tf_op jit(solution)/shard_map/jit(_roll_dynamic)/concatenate | solution.py:26
  174.8 14.4 %pad_maximum_fusion = f32[286,2,4096]{2,1,0:T(2,128)} fusion(f32[254,2,4096]{2,1,0:T(2,128)S(1)} %bitcast.36, f32[32,2,4096]{2,1,0:T(2,128)S(1)} %copy-done), kind=kLoop, calls=%fused_computation.13 | loop fusion | flops 2342912 | bytes 18743296 | tf_op jit(solution)/shard_map/concatenate | solution.py:28
  189.2 18.0 %gather_fusion.1 = f32[224,2,4096]{2,1,0:T(2,128)} fusion(f32[286,2,4096]{2,1,0:T(2,128)} %pad_maximum_fusion, s32[1024]{0:T(1024)S(1)} %pad_clamp_fusion), kind=kCustom, calls=%fused_computation.1 | custom fusion | bytes 14680960 | tf_op jit(solution)/shard_map/gather | solution.py:29
  207.2 14.3 %reshape.103 = f32[32,7,2,64,64]{4,3,2,1,0:T(8,128)} reshape(f32[224,2,4096]{2,1,0:T(2,128)} %gather_fusion.1) | data formatting | bytes 14680064 | tf_op jit(solution)/shard_map/reshape | solution.py:29
  221.6 26.4 %fusion.9 = f32[32,7,2,64,64]{4,3,2,1,0:T(8,128)S(1)} fusion(f32[32,7,2,64,64]{4,3,2,1,0:T(8,128)} %reshape.103, f32[32,7,64,64]{3,2,0,1:T(8,128)} %reshape.75), kind=kOutput, calls=%fused_computation.18 | convolution fusion | flops 1409286144 | bytes 18350080 | tf_op jit(solution)/shard_map/ikxy,ikqyz->ikqxz/dot_general | solution.py:30
  248.0 27.0 %fusion.2 = f32[32,2,7,2,64,64]{4,5,1,3,2,0:T(8,128)} fusion(f32[32,7,2,64,64]{4,3,2,1,0:T(8,128)S(1)} %fusion.9, f32[32,2,64,64]{3,2,1,0:T(8,128)S(1)} %reshape.76, f32[32]{0:T(128)S(1)} %compare_convert_fusion), kind=kOutput, calls=%fused_computation.12 | convolution fusion | flops 2818834432 | bytes 23068800 | tf_op jit(solution)/shard_map/ipyx,ikqyz->ipkqxz/dot_general | solution.py:31
  274.9 30.9 %copy.32 = f32[32,2,7,2,64,64]{5,4,3,2,1,0:T(8,128)} copy(f32[32,2,7,2,64,64]{4,5,1,3,2,0:T(8,128)} %fusion.2) | data formatting | bytes 29360128 | tf_op jit(solution)/shard_map/ipyx,ikqyz->ipkqxz/transpose | solution.py:31
  305.9 24.8 %reshape.102 = f32[896,4096,1]{1,0,2:T(8,128)} reshape(f32[32,2,7,2,64,64]{5,4,3,2,1,0:T(8,128)} %copy.32) | data formatting | bytes 29360128 | tf_op jit(solution)/shard_map/reshape | solution.py:34
  330.7 19.6 %fusion.13 = f32[128,4,4096]{2,0,1:T(8,128)} fusion(f32[896,4096,1]{1,0,2:T(8,128)} %reshape.102, s32[896]{0:T(1024)S(1)} %eq.52, s32[128,4]{0,1:T(4,128)S(1)} %multiply_add_fusion), kind=kOutput, calls=%fused_computation.22 | convolution fusion | flops 22549037056 | bytes 23074304 | tf_op jit(solution)/shard_map/dot_general | solution.py:34
  350.3 9.8 %fusion.6 = f32[128,4,4096]{2,0,1:T(8,128)} fusion(s32[]{:T(128)S(6)} %select_n.37, f32[128,4,4096]{2,0,1:T(8,128)} %fusion.13), kind=kLoop, calls=%fused_computation.15 | loop fusion | flops 2097152 | bytes 16777220 | tf_op jit(solution)/shard_map/jit(_roll_dynamic)/concatenate | solution.py:36
  360.1 12.0 %copy.33 = f32[128,4,4096]{2,1,0:T(4,128)} copy(f32[128,4,4096]{2,0,1:T(8,128)} %fusion.6) | data formatting | bytes 16777216 | tf_op jit(solution)/shard_map/jit(_roll_dynamic)/dynamic_slice | solution.py:36
  372.1 12.4 %all-to-all-start.1 = ((f32[128,4,4096]{2,1,0:T(4,128)}), f32[128,4,4096]{2,1,0:T(4,128)}, u32[]{:S(2)}, u32[]{:S(2)}) async-start(f32[128,4,4096]{2,1,0:T(4,128)} %copy.33), calls=%async_computation.1 | async-start | bytes 16777216 | tf_op jit(solution)/shard_map/all_to_all | solution.py:37
  384.8 100.9 %all-to-all-done.1 = f32[128,4,4096]{2,1,0:T(4,128)} async-done(((f32[128,4,4096]{2,1,0:T(4,128)}), f32[128,4,4096]{2,1,0:T(4,128)}, u32[]{:S(2)}, u32[]{:S(2)}) %all-to-all-start.1) | async-done | bytes 8388640 | tf_op jit(solution)/shard_map/all_to_all | solution.py:37
  485.7 7.7 %rev.7 = f32[128,4,4096]{2,1,0:T(4,128)} reverse(f32[128,4,4096]{2,1,0:T(4,128)} %all-to-all-done.1), dimensions={0} | reverse | bytes 16777216 | tf_op jit(solution)/shard_map/rev | solution.py:38
  493.4 10.8 %fusion.5 = f32[128,4,4096]{2,1,0:T(4,128)} fusion(s32[]{:T(128)S(6)} %select_n.39, f32[128,4,4096]{2,1,0:T(4,128)} %rev.7), kind=kLoop, calls=%fused_computation.14 | loop fusion | flops 2097152 | bytes 16777220 | tf_op jit(solution)/shard_map/jit(_roll_dynamic)/concatenate | solution.py:38
  504.1 10.0 %reshape.78 = f32[512,4096]{1,0:T(8,128)} reshape(f32[128,4,4096]{2,1,0:T(4,128)} %fusion.5) | data formatting | bytes 16777216 | tf_op jit(solution)/shard_map/reshape | solution.py:42
  514.1 6.8 %fusion.18 = f32[8,4096]{1,0:T(8,128)} fusion(f32[512,4096]{1,0:T(8,128)} %reshape.78, s32[512]{0:T(512)S(1)} %eq.45), kind=kOutput, calls=%fused_computation.28 | convolution fusion | flops 201330688 | bytes 8521728 | tf_op jit(solution)/shard_map/dot_general | solution.py:41
  (22 shorter events, 2.7 us)
Async XLA Ops:
  32.7 12.3 %copy-start = (f32[32,2,4096]{2,1,0:T(2,128)S(1)}, f32[32,2,4096]{2,1,0:T(2,128)}, u32[]{:S(2)}) copy-start(f32[32,2,4096]{2,1,0:T(2,128)} %param.12) | copy-start | bytes 3145732
  32.7 13.5 %copy-start.2 = (s32[32,7]{0,1:T(8,128)S(1)}, s32[32,7]{0,1:T(8,128)}, u32[]{:S(2)}) copy-start(s32[32,7]{0,1:T(8,128)} %param.13) | copy-start | bytes 2692
  32.7 113.4 %all-to-all-start = ((f32[128,2,2,4096]{3,2,1,0:T(2,128)}), f32[128,2,2,4096]{3,2,1,0:T(2,128)}, u32[]{:S(2)}, u32[]{:S(2)}) async-start(f32[128,2,2,4096]{3,2,1,0:T(2,128)} %fusion.7), calls=%async_computation | async-start | bytes 16777216 | tf_op jit(solution)/shard_map/all_to_all | solution.py:25
  45.0 9.1 %copy-start.1 = (s32[32,28]{1,0:T(8,128)S(1)}, s32[32,28]{1,0:T(8,128)}, u32[]{:S(2)}) copy-start(s32[32,28]{1,0:T(8,128)} %param.16) | copy-start | bytes 10756
  372.1 12.5 %copy-start.3 = (s32[1,128,4]{1,2,0:T(4,128)S(1)}, s32[1,128,4]{1,2,0:T(4,128)}, u32[]{:S(2)}) copy-start(s32[1,128,4]{1,2,0:T(4,128)} %param.17) | copy-start | bytes 6148
  372.1 113.5 %all-to-all-start.1 = ((f32[128,4,4096]{2,1,0:T(4,128)}), f32[128,4,4096]{2,1,0:T(4,128)}, u32[]{:S(2)}, u32[]{:S(2)}) async-start(f32[128,4,4096]{2,1,0:T(4,128)} %copy.33), calls=%async_computation.1 | async-start | bytes 16777216 | tf_op jit(solution)/shard_map/all_to_all | solution.py:37
where the time goes:
time: 531 us; the launch traced here: 521 us
  waiting for transfers between devices  193 us (36%)
  local copies, waits for them, and re-layouts  157 us (30%)
  matrix products  79.8 us (15%)
  other arithmetic  65.6 us (12%)
  starting transfers between devices  24.7 us (5%)
    all_to_all x1, waiting for transfers between devices, body(): lax.all_to_all(tile_buffer, 'elem', split_axis=0, concat_axis=0, tiled=True)  101 us
    all_to_all x1, waiting for transfers between devices, body(): lax.all_to_all(buffer, 'elem', split_axis=0, concat_axis=0, tiled=True)  91.8 us
    transpose x1, local copies, waits for them, and re-layouts, body(): jnp.einsum('ipyx,ikqyz->ipkqxz', p_masked, product, precision=lax.Precisi...  30.9 us
    dot_general x1, matrix products, body(): jnp.einsum('ipyx,ikqyz->ipkqxz', p_masked, product, precision=lax.Precisi...  27 us
    dot_general x1, matrix products, body(): jnp.einsum('ikxy,ikqyz->ikqxz', a_tiles, neigh, precision=lax.Precision.H...  26.4 us
    reshape x1, local copies, waits for them, and re-layouts, body(): part.reshape(-1, B * B)  24.8 us
    concatenate x1, other arithmetic, body(): back_order = jnp.roll(arrived[::-1], myself + 1, axis=0)  19.7 us
    dot_general x1, matrix products, body(): jnp.dot(slot_table, part.reshape(-1, B * B), precision=lax.Precision.HIGH...  19.6 us
  transfers between devices with their start and end apart: 2, of which 2 were waited for; matrix products, arithmetic and copies ran while one was open for 2% of the time, Pallas kernels for 0%

commit v1 on v0

v1 whole, which is shorter than its diff:
```python
import jax
import jax.numpy as jnp
from jax import lax
from jax.experimental import pallas as pl
from jax.experimental.pallas import tpu as pltpu
from jax.sharding import PartitionSpec as P

B = 64
KA = 7
KP = 2
S = 2
CAP = 4
TO = 8
R = 32
N = 128
RING = 4
LANES = 128
TILE_ROWS = B * B // LANES
OWNER_ROWS = TO * TILE_ROWS
EXT = R + N * S
MESH = pl.DeviceIdType.MESH

GROUPS = ((0, 88), (88, 88), (176, 80))
ORDERS = ((0, 1, 2), (1, 2, 0), (2, 0, 1))


def serve_kernel(index_ref, rows_ref, out_ref, sem):
    def send(n, carry):
        pltpu.make_async_copy(rows_ref.at[index_ref[n]], out_ref.at[n], sem).start()
        return carry

    lax.fori_loop(0, N * S, send, 0)
    pltpu.make_async_copy(out_ref, out_ref, sem).wait()


def split(value):
    high = value.astype(jnp.bfloat16)
    low = (value - high.astype(jnp.float32)).astype(jnp.bfloat16)
    return high, low


def left_kernel(count_ref, p_ref, a_ref, out_ref):
    row = pl.program_id(0)
    high, low = split(p_ref[0].T)
    left = jnp.concatenate([high, low], axis=1)
    lane = lax.broadcasted_iota(jnp.int32, (KP * B, LANES), 1)
    for k in range(KA):
        a_high, a_low = split(a_ref[0, k])
        wide = jnp.concatenate([a_high, a_low], axis=1)
        both = jnp.dot(left, jnp.concatenate([wide, wide], axis=0), preferred_element_type=jnp.float32)
        twice = both + pltpu.roll(both, B, 1)
        twice = jnp.where(row < count_ref[0], twice, 0.0)
        m_high = twice.astype(jnp.bfloat16).astype(jnp.float32)
        out_ref[0, k] = jnp.where(lane < B, m_high, twice - m_high).astype(jnp.bfloat16)


def tile_kernel(index_ref, slot_ref, table_ref, m_ref, own_ref, far_ref, out_ref, ext, acc, load_sem, out_sem):
    row = pl.program_id(0)

    @pl.when(row == 0)
    def _():
        own = pltpu.make_async_copy(own_ref, ext.at[pl.ds(0, R)], load_sem.at[0])
        far = pltpu.make_async_copy(far_ref, ext.at[pl.ds(R, N * S)], load_sem.at[1])
        own.start()
        far.start()

        def clear(n, carry):
            acc[pl.ds(n * 8, 8)] = jnp.zeros((8, TILE_ROWS, LANES), jnp.float32)
            return carry

        lax.fori_loop(0, N * TO // 8, clear, 0)
        own.wait()
        far.wait()

    lane = lax.broadcasted_iota(jnp.int32, (TILE_ROWS, LANES), 1)
    for k in range(KA):
        high, low = split(ext[index_ref[row * KA + k]])
        wide = jnp.concatenate([high, low], axis=1)
        both = jnp.dot(m_ref[0, k], jnp.concatenate([wide, wide], axis=0), preferred_element_type=jnp.float32)
        part = both[:, :LANES] + both[:, LANES:]
        turned = pltpu.roll(part, B, 1)
        for p in range(KP):
            top, bottom = p * B, p * B + TILE_ROWS
            upper, lower = part[top : top + TILE_ROWS], part[bottom : bottom + TILE_ROWS]
            upper_t, lower_t = turned[top : top + TILE_ROWS], turned[bottom : bottom + TILE_ROWS]
            tiles = (jnp.where(lane < B, upper, lower_t), jnp.where(lane < B, upper_t, lower))
            for q in range(KP):
                target = table_ref[slot_ref[row * (KP * KA * KP) + p * (KA * KP) + k * KP + q]]
                acc[target] += tiles[q]

    @pl.when(row == R - 1)
    def _():
        done = pltpu.make_async_copy(acc, out_ref, out_sem)
        done.start()
        done.wait()


def ring_shapes():
    shapes = []
    for _, length in GROUPS:
        for stage in range(3):
            lead = (RING,) * (2 - stage)
            slab = lead + (length, LANES)
            shapes += [pltpu.VMEM(slab, jnp.float32)] * 3
    return shapes


def add(target, *terms):
    lead = target.shape[:-2]
    total = 1
    for size in lead:
        total *= size

    def one(n, carry):
        at = []
        for size in reversed(lead):
            at.insert(0, n % size)
            n = n // size
        at = tuple(at) + (slice(None), slice(None))
        value = target[at]
        for term in terms:
            value = value + term[at]
        target[at] = value
        return carry

    if total == 1:
        one(0, 0)
    else:
        lax.fori_loop(0, total, one, 0)


def reduce_kernel(acc_ref, out_ref, mine, theirs, *rest):
    bufs, (in_send, in_recv, in_load, ring_send, ring_recv) = rest[:27], rest[27:]
    me = lax.axis_index("elem")
    core = me % 2
    chip = me // 2
    place = (chip // (RING * RING), (chip // RING) % RING, chip % RING)
    partner = me + 1 - 2 * core

    def device_at(axis, step):
        at = list(place)
        at[axis] = (at[axis] + step) % RING
        return ((at[0] * RING + at[1]) * RING + at[2]) * 2 + core

    barrier = pltpu.get_barrier_semaphore()
    near = [partner] + [device_at(axis, step) for axis in range(3) for step in (1, 3)]
    for other in near:
        pl.semaphore_signal(barrier, inc=1, device_id=(other,), device_id_type=MESH)
    pl.semaphore_wait(barrier, len(near))

    def window(group, fixed, part):
        free = [axis for axis in range(3) if axis not in fixed]
        at = [fixed.get(axis, slice(None)) for axis in range(3)]
        inner = [slice(None)] * len(free)
        first, length = GROUPS[group]
        rows = (0, length)
        if part is not None:
            if free:
                at[free[0]] = inner[0] = pl.ds(part * (RING // 2), RING // 2)
            else:
                half = (length + 8) // 16 * 8
                rows = (half * part, length - half if part else half)
        return (
            tuple(at) + (pl.ds(first + rows[0], rows[1]), slice(None)),
            tuple(inner) + (pl.ds(rows[0], rows[1]), slice(None)),
        )

    def across(group, fixed, core_at):
        at, _ = window(group, fixed, None)
        return at[:3] + (core_at,) + at[3:]

    loads = {}
    for offset in (2, 1, 3, 0):
        for group in range(3):
            axis = ORDERS[group][0]
            fixed = {axis: (place[axis] + offset) % RING}
            n = group * RING + offset
            at, _ = window(group, fixed, None)
            give = pltpu.make_async_remote_copy(
                src_ref=acc_ref.at[across(group, fixed, 1 - core)],
                dst_ref=theirs.at[at],
                send_sem=in_send.at[n],
                recv_sem=in_recv.at[n],
                device_id=(partner,),
                device_id_type=MESH,
            )
            keep = pltpu.make_async_copy(acc_ref.at[across(group, fixed, core)], mine.at[at], in_load.at[n])
            give.start()
            keep.start()
            loads[group, offset] = (give, keep, at)

    def arrive(group, offset):
        give, keep, at = loads[group, offset]
        keep.wait()
        give.wait_recv()
        add(mine.at[at], theirs.at[at])

    sends = [give for give, _, _ in loads.values()]
    flights = {}

    def fixed_at(group, stage, step):
        order = ORDERS[group]
        fixed = {axis: place[axis] for axis in order[:stage]}
        fixed[order[stage]] = (place[order[stage]] + step) % RING
        return fixed

    def start(group, stage, kind, step, part, towards, buffer):
        n = (group * 3 + stage) * 6 + kind
        at, inner = window(group, fixed_at(group, stage, step), part)
        copy = pltpu.make_async_remote_copy(
            src_ref=mine.at[at],
            dst_ref=bufs[(group * 3 + stage) * 3 + buffer].at[inner],
            send_sem=ring_send.at[n],
            recv_sem=ring_recv.at[n],
            device_id=(device_at(ORDERS[group][stage], towards),),
            device_id_type=MESH,
        )
        copy.start()
        flights[group, stage, kind] = copy
        sends.append(copy)

    def first_wave(group, stage):
        if stage == 0:
            arrive(group, 2)
        start(group, stage, 0, 2, 0, 1, 0)
        start(group, stage, 1, 2, 1, 3, 0)
        if stage == 0:
            arrive(group, 1)
        start(group, stage, 2, 1, 1, 1, 1)
        if stage == 0:
            arrive(group, 3)
        start(group, stage, 3, 3, 0, 3, 2)

    def second_wave(group, stage):
        buffer = bufs[(group * 3 + stage) * 3]
        for kind, part, step in ((0, 0, 1), (1, 1, 3)):
            flights[group, stage, kind].wait_recv()
            at, inner = window(group, fixed_at(group, stage, step), part)
            add(mine.at[at], buffer.at[inner])
            start(group, stage, 4 + kind, step, part, step, 1 + kind)

    def third_wave(group, stage):
        for kind in (2, 3, 4, 5):
            flights[group, stage, kind].wait_recv()
        at, _ = window(group, fixed_at(group, stage, 0), None)
        _, plus, minus = bufs[(group * 3 + stage) * 3 : (group * 3 + stage) * 3 + 3]
        if stage < 2:
            add(mine.at[at], plus, minus)
        else:
            first, length = GROUPS[group]
            out_ref[pl.ds(first, length), :] = mine[at] + plus[...] + minus[...]

    for group in range(3):
        first_wave(group, 0)
    for stage in range(3):
        for group in range(3):
            second_wave(group, stage)
        for group in range(3):
            if stage == 0:
                arrive(group, 0)
            third_wave(group, stage)
            if stage < 2:
                first_wave(group, stage + 1)
    for copy in sends:
        copy.wait_send()


def reduce_scatter(acc):
    return pl.pallas_call(
        reduce_kernel,
        out_shape=jax.ShapeDtypeStruct((OWNER_ROWS, LANES), jnp.float32),
        in_specs=[pl.BlockSpec(memory_space=pl.ANY)],
        out_specs=pl.BlockSpec(memory_space=pltpu.VMEM),
        scratch_shapes=[
            pltpu.VMEM((RING, RING, RING, OWNER_ROWS, LANES), jnp.float32),
            pltpu.VMEM((RING, RING, RING, OWNER_ROWS, LANES), jnp.float32),
            *ring_shapes(),
            pltpu.SemaphoreType.DMA((12,)),
            pltpu.SemaphoreType.DMA((12,)),
            pltpu.SemaphoreType.DMA((12,)),
            pltpu.SemaphoreType.DMA((54,)),
            pltpu.SemaphoreType.DMA((54,)),
        ],
        compiler_params=pltpu.CompilerParams(collective_id=0, has_side_effects=True, vmem_limit_bytes=48 * 2**20),
        name="reduce_scatter",
    )(acc.reshape(RING, RING, RING, 2, OWNER_ROWS, LANES))


def body(a_blocks, p_blocks, a_slot, serve_rows, row_count, contrib_slot, recv_tile):
    me = lax.axis_index("elem")
    every = jnp.arange(N, dtype=jnp.int32)
    rows = p_blocks.reshape(R, KP, B, B).transpose(0, 2, 1, 3).reshape(R, B, LANES)

    by_offset = jnp.concatenate([jnp.zeros((1, S), jnp.int32), serve_rows[0]], axis=0)
    serve_index = jnp.roll(by_offset, me, axis=0).reshape(N * S)
    outgoing = pl.pallas_call(
        serve_kernel,
        grid_spec=pltpu.PrefetchScalarGridSpec(
            num_scalar_prefetch=1,
            in_specs=[pl.BlockSpec(memory_space=pltpu.VMEM)],
            out_specs=pl.BlockSpec(memory_space=pl.ANY),
            scratch_shapes=[pltpu.SemaphoreType.DMA],
        ),
        out_shape=jax.ShapeDtypeStruct((N * S, B, LANES), jnp.float32),
        name="serve",
    )(serve_index, rows)
    arrived = lax.all_to_all(outgoing, "elem", split_axis=0, concat_axis=0, tiled=True)

    back = jnp.roll(recv_tile[0][::-1], me + 1, axis=0)
    told = lax.all_to_all(back, "elem", split_axis=0, concat_axis=0, tiled=True)
    table = jnp.roll(told + every[:, None] * TO, -me, axis=0).reshape(N * CAP)

    left = pl.pallas_call(
        left_kernel,
        grid_spec=pltpu.PrefetchScalarGridSpec(
            num_scalar_prefetch=1,
            grid=(R,),
            in_specs=[
                pl.BlockSpec((1, B, LANES), lambda i, c: (i, 0, 0)),
                pl.BlockSpec((1, KA, B, B), lambda i, c: (i, 0, 0, 0)),
            ],
            out_specs=pl.BlockSpec((1, KA, KP * B, LANES), lambda i, c: (i, 0, 0, 0)),
        ),
        out_shape=jax.ShapeDtypeStruct((R, KA, KP * B, LANES), jnp.bfloat16),
        cost_estimate=pl.CostEstimate(flops=4 * 2 * R * KA * 128 * 64 * 64, bytes_accessed=16 * 2**20, transcendentals=0),
        name="left_products",
    )(row_count, rows, a_blocks.reshape(R, KA, B, B))

    slot = a_slot.reshape(R * KA)
    source = lax.rem(me + (2 * N - 1) - (slot - R) // S, N)
    ext_index = jnp.where(slot < R, slot, R + source * S + (slot - R) % S)
    acc = pl.pallas_call(
        tile_kernel,
        grid_spec=pltpu.PrefetchScalarGridSpec(
            num_scalar_prefetch=3,
            grid=(R,),
            in_specs=[
                pl.BlockSpec((1, KA, KP * B, LANES), lambda i, a, b, c: (i, 0, 0, 0)),
                pl.BlockSpec(memory_space=pl.ANY),
                pl.BlockSpec(memory_space=pl.ANY),
            ],
            out_specs=pl.BlockSpec(memory_space=pl.ANY),
            scratch_shapes=[
                pltpu.VMEM((EXT, B, LANES), jnp.float32),
                pltpu.VMEM((N * TO, TILE_ROWS, LANES), jnp.float32),
                pltpu.SemaphoreType.DMA((2,)),
                pltpu.SemaphoreType.DMA,
            ],
        ),
        out_shape=jax.ShapeDtypeStruct((N * TO, TILE_ROWS, LANES), jnp.float32),
        compiler_params=pltpu.CompilerParams(vmem_limit_bytes=40 * 2**20),
        cost_estimate=pl.CostEstimate(flops=4 * 2 * R * KA * 128 * 64 * 128, bytes_accessed=34 * 2**20, transcendentals=0),
        name="tiles",
    )(ext_index, contrib_slot.reshape(-1), table, left, rows, arrived)

    tiles = reduce_scatter(acc)
    return tiles.reshape(TO, TILE_ROWS, 2, B).transpose(0, 2, 1, 3).reshape(TO, B * B)


def solution(mesh):
    in_specs = (
        P("elem", None, None),
        P("elem", None, None),
        P("elem", None),
        P("elem", None, None),
        P("elem"),
        P("elem", None),
        P("elem", None, None),
    )
    return jax.shard_map(body, mesh=mesh, in_specs=in_specs, out_specs=P("elem", None), check_vma=False)
```

time: 531 us -> 225 us (0.42); the launches traced: 521 us -> 223 us
  waiting for transfers between devices: 193 us -> 59.4 us
  local copies, waits for them, and re-layouts: 157 us -> 30.1 us
  Pallas kernels: 0 us -> 110 us
  matrix products: 79.8 us -> 0 us
  other arithmetic: 65.6 us -> 1.04 us
    all_to_all x2, waiting for transfers between devices: 193 us -> 59.4 us  [the longest x1 59.4 us: body(): lax.all_to_all(outgoing, 'elem', split_axis=0, concat_axis=0, tiled=True)]
    pallas_call x0 -> x4, Pallas kernels: none -> 110 us  [the longest x1 55.4 us: reduce_scatter(): pl.pallas_call(reduce_kernel, out_shape=jax.ShapeDtypeStruct((OWNER_ROWS,...]
    dot_general x4 -> x0, matrix products: 79.8 us -> none  [the longest x1 27 us: body(): jnp.einsum('ipyx,ikqyz->ipkqxz', p_masked, product, precision=lax.Precisi...]
    concatenate x5 -> x2, other arithmetic: 64.9 us -> 0.94 us  [the longest x1 0.84 us: body(): serve_index = jnp.roll(by_offset, me, axis=0).reshape(N * S)]
    gather x2 -> x0, local copies, waits for them, and re-layouts: 33.9 us -> none  [the longest x1 18 us: body(): neigh = extended[a_slot].reshape(rows, KA, KP, B, B)]
    reshape x5 -> x11, local copies, waits for them, and re-layouts: 57.3 us -> 25.1 us  [the longest x2 14.5 us: body(): a_blocks.reshape(R, KA, B, B)]
    transpose x1, local copies, waits for them, and re-layouts: 30.9 us -> 0.02 us  [body(): tiles.reshape(TO, TILE_ROWS, 2, B).transpose(0, 2, 1, 3).reshape(TO, B * B)]
    rev x2 -> x1, local copies, waits for them, and re-layouts: 16.8 us -> 0.77 us  [body(): back = jnp.roll(recv_tile[0][::-1], me + 1, axis=0)]
  transfers between devices with their start and end apart: 2 -> 2, of which waited for: 2 -> 1; matrix products, arithmetic and copies ran while one was open for 2% -> 11% of each run, Pallas kernels for 0% -> 14%
where the time goes in v1:
time: 225 us; the launch traced here: 223 us
  Pallas kernels  110 us (49%)
  waiting for transfers between devices  59.4 us (26%)
  local copies, waits for them, and re-layouts  30.1 us (13%)
  starting transfers between devices  21.7 us (10%)
    all_to_all x1, waiting for transfers between devices, body(): lax.all_to_all(outgoing, 'elem', split_axis=0, concat_axis=0, tiled=True)  59.4 us
    pallas_call x1, Pallas kernels, reduce_scatter(): pl.pallas_call(reduce_kernel, out_shape=jax.ShapeDtypeStruct((OWNER_ROWS,...  55.4 us
    pallas_call x1, Pallas kernels, body(): pl.pallas_call(left_kernel, grid_spec=pltpu.PrefetchScalarGridSpec(num_sc...  26.1 us
    pallas_call x1, Pallas kernels, body(): pl.pallas_call(tile_kernel, grid_spec=pltpu.PrefetchScalarGridSpec(num_sc...  23 us
    reshape x2, local copies, waits for them, and re-layouts, body(): a_blocks.reshape(R, KA, B, B)  14.5 us
    all_to_all x1, starting transfers between devices, body(): told = lax.all_to_all(back, 'elem', split_axis=0, concat_axis=0, tiled=True)  11.5 us
    all_to_all x1, starting transfers between devices, body(): lax.all_to_all(outgoing, 'elem', split_axis=0, concat_axis=0, tiled=True)  10.2 us
    reshape x3, local copies, waits for them, and re-layouts, body(): p_blocks.reshape(R, KP, B, B).transpose(0, 2, 1, 3).reshape(R, B, LANES)  8.62 us
  transfers between devices with their start and end apart: 2, of which 1 were waited for; matrix products, arithmetic and copies ran while one was open for 11% of the time, Pallas kernels for 14%

profile of v1, /device:TPU:1, one launch (start us, length us, event | category | flops | bytes accessed | tf_op | source)
XLA Modules:
  0.0 222.8 jit_solution(3468038569343903567)
XLA Ops:
  0.0 0.8 rev.3
  0.8 0.7 copy.38
  1.6 11.5 %all-to-all-start = ((s32[128,1,4]{2,1,0:T(1,128)}), s32[128,1,4]{2,1,0:T(1,128)S(1)}, u32[]{:S(2)}, u32[]{:S(2)}) async-start(s32[128,1,4]{2,1,0:T(1,128)} %copy.38), calls=%async_computation | async-start | bytes 131072 | tf_op jit(solution)/shard_map/all_to_all | solution.py:310
  13.1 0.8 fusion.6
  14.0 0.1 copy.43
  14.1 0.7 reshape.43.index_ref
  14.8 3.2 %reshape.40 = f32[32,2,64,64]{3,2,1,0:T(8,128)} reshape(f32[32,2,4096]{2,1,0:T(2,128)} %param.10) | data formatting | bytes 2097152 | tf_op jit(solution)/shard_map/reshape | solution.py:292
  18.0 3.3 %copy.46 = f32[32,2,64,64]{3,1,2,0:T(2,128)S(1)} copy(f32[32,2,64,64]{3,2,1,0:T(8,128)} %reshape.40) | data formatting | bytes 2097152 | tf_op jit(solution)/shard_map/reshape | solution.py:292
  21.3 2.1 reshape.41.p_ref.rows_ref.own_ref
  23.4 5.2 %serve.1 = f32[256,64,128]{2,1,0:T(8,128)} custom-call(s32[256]{0:T(256)} %reshape.43.index_ref, f32[32,64,128]{2,1,0:T(8,128)} %reshape.41.p_ref.rows_ref.own_ref), custom_call_target="tpu_custom_call" | custom-call | tf_op jit(solution)/shard_map/serve/pallas_call | solution.py:296
  28.6 10.2 %all-to-all-start.1 = ((f32[256,64,128]{2,1,0:T(8,128)}), f32[256,64,128]{2,1,0:T(8,128)}, u32[]{:S(2)}, u32[]{:S(2)}) async-start(f32[256,64,128]{2,1,0:T(8,128)} %serve.1), calls=%async_computation.1 | async-start | bytes 16777216 | tf_op jit(solution)/shard_map/all_to_all | solution.py:307
  39.5 0.1 reshape.38.slot_ref
  39.7 0.1 reshape.37
  39.8 7.0 %reshape.42 = f32[32,7,64,64]{3,2,0,1:T(8,128)} reshape(f32[32,7,4096]{2,0,1:T(8,128)} %param.9) | data formatting | bytes 7340032 | tf_op jit(solution)/shard_map/reshape | solution.py:327
  46.9 7.5 %copy.42.a_ref = f32[32,7,64,64]{3,2,1,0:T(8,128)} copy(f32[32,7,64,64]{3,2,0,1:T(8,128)} %reshape.42) | data formatting | bytes 7340032 | tf_op jit(solution)/shard_map/reshape | solution.py:327
  54.4 26.1 %left_products.1.m_ref = bf16[32,7,128,128]{3,2,1,0:T(8,128)(2,1)} custom-call(s32[1]{0:T(128)S(6)} %copy.47.count_ref, f32[32,64,128]{2,1,0:T(8,128)} %reshape.41.p_ref.rows_ref.own_ref, f32[32,7,64,64]{3,2,1,0:T(8,128)} %copy.42.a_ref), custom_call_target="tpu_custom_call" | custom-call | flops 939524096 | bytes 16777216 | tf_op jit(solution)/shard_map/left_products/pallas_call | solution.py:313
  80.7 0.1 copy.40
  80.8 0.1 reshape.39.table_ref
  80.9 59.4 %all-to-all-done.1.far_ref = f32[256,64,128]{2,1,0:T(8,128)} async-done(((f32[256,64,128]{2,1,0:T(8,128)}), f32[256,64,128]{2,1,0:T(8,128)}, u32[]{:S(2)}, u32[]{:S(2)}) %all-to-all-start.1) | async-done | bytes 8388640 | tf_op jit(solution)/shard_map/all_to_all | solution.py:307
  140.3 3.1 %copy-done = bf16[32,7,128,128]{3,2,1,0:T(8,128)(2,1)S(1)} copy-done((bf16[32,7,128,128]{3,2,1,0:T(8,128)(2,1)S(1)}, bf16[32,7,128,128]{3,2,1,0:T(8,128)(2,1)}, u32[]{:S(2)}) %copy-start) | copy-done | bytes 7340056
  143.4 23.0 %tiles.1 = f32[1024,32,128]{2,1,0:T(8,128)} custom-call(s32[224]{0:T(256)S(1)} %compare_select_fusion.index_ref, s32[896]{0:T(1024)S(1)} %reshape.38.slot_ref, s32[512]{0:T(512)S(1)} %reshape.39.table_ref, bf16[32,7,128,128]{3,2,1,0:T(8,128)(2,1)S(1)} %copy-done, f32[32,64,128]{2,1,0:T(8,128)S(1)} %copy-done.1, f32[256,64,128]{2,1,0:T(8,128)} %all-to-all-done.1.far_ref), custom_call_target="tpu_custom_call" | custom-call | flops 1879048192 | bytes 35651584 | tf_op jit(solution)/shard_map/tiles/pallas_call | solution.py:332
  166.4 55.4 %reduce_scatter.1 = f32[256,128]{1,0:T(8,128)S(1)} custom-call(f32[4,4,4,2,256,128]{5,4,3,2,1,0:T(8,128)} %bitcast.15), custom_call_target="tpu_custom_call" | custom-call | tf_op jit(solution)/shard_map/reduce_scatter/pallas_call | solution.py:269
  221.8 0.2 reshape.45
  222.0 0.8 reshape.46
  (17 shorter events, 0.4 us)
Async XLA Ops:
  1.6 27.0 %all-to-all-start = ((s32[128,1,4]{2,1,0:T(1,128)}), s32[128,1,4]{2,1,0:T(1,128)S(1)}, u32[]{:S(2)}, u32[]{:S(2)}) async-start(s32[128,1,4]{2,1,0:T(1,128)} %copy.38), calls=%async_computation | async-start | bytes 131072 | tf_op jit(solution)/shard_map/all_to_all | solution.py:310
  28.6 10.9 %copy-start.2 = (s32[32,28]{1,0:T(8,128)S(1)}, s32[32,28]{1,0:T(8,128)}, u32[]{:S(2)}) copy-start(s32[32,28]{1,0:T(8,128)} %param.14) | copy-start | bytes 10756
  28.6 11.0 %copy-start.3 = (s32[32,7]{0,1:T(8,128)S(1)}, s32[32,7]{0,1:T(8,128)}, u32[]{:S(2)}) copy-start(s32[32,7]{0,1:T(8,128)} %param.11) | copy-start | bytes 2692
  28.6 111.7 %all-to-all-start.1 = ((f32[256,64,128]{2,1,0:T(8,128)}), f32[256,64,128]{2,1,0:T(8,128)}, u32[]{:S(2)}, u32[]{:S(2)}) async-start(f32[256,64,128]{2,1,0:T(8,128)} %serve.1), calls=%async_computation.1 | async-start | bytes 16777216 | tf_op jit(solution)/shard_map/all_to_all | solution.py:307
  54.4 86.0 %copy-start.1 = (f32[32,64,128]{2,1,0:T(8,128)S(1)}, f32[32,64,128]{2,1,0:T(8,128)}, u32[]{:S(2)}) copy-start(f32[32,64,128]{2,1,0:T(8,128)} %reshape.41.p_ref.rows_ref.own_ref) | copy-start | bytes 3145732
  140.3 3.1 %copy-start = (bf16[32,7,128,128]{3,2,1,0:T(8,128)(2,1)S(1)}, bf16[32,7,128,128]{3,2,1,0:T(8,128)(2,1)}, u32[]{:S(2)}) copy-start(bf16[32,7,128,128]{3,2,1,0:T(8,128)(2,1)} %left_products.1.m_ref) | copy-start | bytes 22020100

commit v2 on v1

v2 whole, which is shorter than its diff:
```python
import jax
import jax.numpy as jnp
from jax import lax
from jax.experimental import pallas as pl
from jax.experimental.pallas import tpu as pltpu
from jax.sharding import PartitionSpec as P


B = 64
KA = 7
KP = 2
S = 2
CAP = 4
TO = 8
R = 32
N = 128
RING = 4
LANES = 128
TILE_ROWS = B * B // LANES
OWNER_ROWS = TO * TILE_ROWS
EXT = R + N * S
PARTS = 4
MESH = pl.DeviceIdType.MESH

GROUPS = ((0, 40), (40, 48), (88, 40), (128, 48), (176, 40), (216, 40))
ORDERS = ((0, 1, 2), (1, 2, 0), (2, 0, 1)) * 2
SETS = ((0, 1, 2), (3, 4, 5))


def serve_kernel(serve_ref, raw_ref, rows_ref, out_ref, sem):
    me = lax.axis_index("elem")
    lane = lax.broadcasted_iota(jnp.int32, (B, LANES), 1) < B
    even = lax.broadcasted_iota(jnp.int32, (B, LANES), 0) % 2 == 0

    def turn(n, carry):
        raw = raw_ref[n]
        halves = pltpu.roll(raw, B, 1)
        other = jnp.where(even, pltpu.roll(halves, B - 1, 0), pltpu.roll(halves, 1, 0))
        rows_ref[n] = jnp.where(lane == even, raw, other)
        return carry

    lax.fori_loop(0, R, turn, 0, unroll=4)

    def send(n, carry):
        to = lax.rem(me + 1 + n, N)
        for c in range(S):
            pltpu.make_async_copy(rows_ref.at[serve_ref[c, n]], out_ref.at[to * S + c], sem).start()
        return carry

    lax.fori_loop(0, N - 1, send, 0)
    for c in range(S):
        pltpu.make_async_copy(rows_ref.at[0], out_ref.at[me * S + c], sem).start()
    pltpu.make_async_copy(out_ref, out_ref, sem).wait()


def table_kernel(tiles_ref, out_ref, send_sem, recv_sem, own_sem):
    me = lax.axis_index("elem")

    def greet(m, carry):
        pl.semaphore_signal(barrier, inc=1, device_id=(lax.rem(me + m, N),), device_id_type=MESH)
        return carry

    def send(m, carry):
        pltpu.make_async_remote_copy(
            src_ref=tiles_ref.at[m],
            dst_ref=out_ref.at[m],
            send_sem=send_sem,
            recv_sem=recv_sem,
            device_id=(lax.rem(me + N - m, N),),
            device_id_type=MESH,
        ).start()
        return carry

    own = pltpu.make_async_copy(tiles_ref.at[0], out_ref.at[0], own_sem)
    own.start()
    barrier = pltpu.get_barrier_semaphore()
    lax.fori_loop(1, N, greet, 0)
    pl.semaphore_wait(barrier, N - 1)
    lax.fori_loop(1, N, send, 0)
    own.wait()
    rest = pl.ds(1, N - 1)
    pltpu.make_async_copy(tiles_ref.at[rest], tiles_ref.at[rest], send_sem).wait()
    pltpu.make_async_copy(out_ref.at[rest], out_ref.at[rest], recv_sem).wait()


def split(value):
    high = value.astype(jnp.bfloat16)
    low = (value - high.astype(jnp.float32)).astype(jnp.bfloat16)
    return high, low


def left_kernel(count_ref, p_ref, a_ref, out_ref):
    row = pl.program_id(0)
    high, low = split(p_ref[row].T)
    left = jnp.concatenate([high, low], axis=1)
    lane = lax.broadcasted_iota(jnp.int32, (KP * B, LANES), 1)
    for k in range(KA):
        a_high, a_low = split(a_ref[0, k])
        wide = jnp.concatenate([a_high, a_low], axis=1)
        both = jnp.dot(left, jnp.concatenate([wide, wide], axis=0), preferred_element_type=jnp.float32)
        twice = both + pltpu.roll(both, B, 1)
        twice = jnp.where(row < count_ref[0], twice, 0.0)
        m_high = twice.astype(jnp.bfloat16).astype(jnp.float32)
        out_ref[0, k] = jnp.where(lane < B, m_high, twice - m_high).astype(jnp.bfloat16)


def tile_kernel(index_ref, slot_ref, table_ref, left_ref, own_ref, far_ref, acc, ext, m_ref, load_sem, left_sem):
    own = pltpu.make_async_copy(own_ref, ext.at[pl.ds(0, R)], load_sem.at[0])
    far = pltpu.make_async_copy(far_ref, ext.at[pl.ds(R, N * S)], load_sem.at[1])
    far.start()
    own.start()
    parts = []
    for n in range(PARTS):
        some = pl.ds(n * (R // PARTS), R // PARTS)
        parts.append(pltpu.make_async_copy(left_ref.at[some], m_ref.at[some], left_sem.at[n]))
        parts[n].start()

    def clear(n, carry):
        acc[pl.ds(n * 8, 8)] = jnp.zeros((8, TILE_ROWS, LANES), jnp.float32)
        return carry

    lax.fori_loop(0, N * TO // 8, clear, 0)
    own.wait()
    far.wait()
    lane = lax.broadcasted_iota(jnp.int32, (TILE_ROWS, LANES), 1)

    def step(row, carry):
        for k in range(KA):
            high, low = split(ext[index_ref[row * KA + k]])
            wide = jnp.concatenate([high, low], axis=1)
            both = jnp.dot(m_ref[row, k], jnp.concatenate([wide, wide], axis=0), preferred_element_type=jnp.float32)
            part = both[:, :LANES] + both[:, LANES:]
            turned = pltpu.roll(part, B, 1)
            for p in range(KP):
                top, bottom = p * B, p * B + TILE_ROWS
                upper, lower = part[top : top + TILE_ROWS], part[bottom : bottom + TILE_ROWS]
                upper_t, lower_t = turned[top : top + TILE_ROWS], turned[bottom : bottom + TILE_ROWS]
                tiles = (jnp.where(lane < B, upper, lower_t), jnp.where(lane < B, upper_t, lower))
                for q in range(KP):
                    target = table_ref[slot_ref[row * (KP * KA * KP) + p * (KA * KP) + k * KP + q]]
                    acc[target] += tiles[q]
        return carry

    for n in range(PARTS):
        parts[n].wait()
        lax.fori_loop(n * (R // PARTS), (n + 1) * (R // PARTS), step, 0)


def ring_shapes():
    shapes = []
    for _, length in GROUPS:
        for stage in range(3):
            lead = (RING,) * (2 - stage)
            slab = lead + (length, LANES)
            shapes += [pltpu.VMEM(slab, jnp.float32)] * 3
    return shapes


def add(target, *terms):
    lead = target.shape[:-2]
    total = 1
    for size in lead:
        total *= size

    def one(n, carry):
        at = []
        for size in reversed(lead):
            at.insert(0, n % size)
            n = n // size
        at = tuple(at) + (slice(None), slice(None))
        value = target[at]
        for term in terms:
            value = value + term[at]
        target[at] = value
        return carry

    if total == 1:
        one(0, 0)
    else:
        lax.fori_loop(0, total, one, 0)


def reduce_kernel(acc_ref, out_ref, mine, *rest):
    bufs, (in_send, in_recv, ring_send, ring_recv) = rest[:-4], rest[-4:]
    me = lax.axis_index("elem")
    core = me % 2
    chip = me // 2
    place = (chip // (RING * RING), (chip // RING) % RING, chip % RING)
    partner = me + 1 - 2 * core

    def device_at(axis, step):
        at = list(place)
        at[axis] = (at[axis] + step) % RING
        return ((at[0] * RING + at[1]) * RING + at[2]) * 2 + core

    barrier = pltpu.get_barrier_semaphore()
    near = [partner] + [device_at(axis, step) for axis in range(3) for step in (1, 3)]
    for other in near:
        pl.semaphore_signal(barrier, inc=1, device_id=(other,), device_id_type=MESH)
    pl.semaphore_wait(barrier, len(near))

    def window(group, fixed, part):
        free = [axis for axis in range(3) if axis not in fixed]
        at = [fixed.get(axis, slice(None)) for axis in range(3)]
        inner = [slice(None)] * len(free)
        first, length = GROUPS[group]
        rows = (0, length)
        if part is not None:
            if free:
                at[free[0]] = inner[0] = pl.ds(part * (RING // 2), RING // 2)
            else:
                half = (length + 8) // 16 * 8
                rows = (half * part, length - half if part else half)
        return (
            tuple(at) + (pl.ds(first + rows[0], rows[1]), slice(None)),
            tuple(inner) + (pl.ds(rows[0], rows[1]), slice(None)),
        )

    def across(group, fixed, core_at):
        at, _ = window(group, fixed, None)
        return at[:3] + (core_at,) + at[3:]

    loads = {}
    for groups, offset in ((0, 2), (0, 1), (0, 3), (1, 2), (1, 1), (1, 3), (0, 0), (1, 0)):
        for group in SETS[groups]:
            axis = ORDERS[group][0]
            fixed = {axis: (place[axis] + offset) % RING}
            n = group * RING + offset
            at, _ = window(group, fixed, None)
            give = pltpu.make_async_remote_copy(
                src_ref=acc_ref.at[across(group, fixed, 1 - core)],
                dst_ref=mine.at[at],
                send_sem=in_send.at[n],
                recv_sem=in_recv.at[n],
                device_id=(partner,),
                device_id_type=MESH,
            )
            give.start()
            loads[group, offset] = (give, acc_ref.at[across(group, fixed, core)], mine.at[at])

    def arrive(group, offset):
        give, own, target = loads[group, offset]
        give.wait_recv()
        add(target, own)

    sends = [give for give, _, _ in loads.values()]
    flights = {}

    def fixed_at(group, stage, step):
        order = ORDERS[group]
        fixed = {axis: place[axis] for axis in order[:stage]}
        fixed[order[stage]] = (place[order[stage]] + step) % RING
        return fixed

    def start(group, stage, kind, step, part, towards, buffer):
        n = (group * 3 + stage) * 6 + kind
        at, inner = window(group, fixed_at(group, stage, step), part)
        copy = pltpu.make_async_remote_copy(
            src_ref=mine.at[at],
            dst_ref=bufs[(group * 3 + stage) * 3 + buffer].at[inner],
            send_sem=ring_send.at[n],
            recv_sem=ring_recv.at[n],
            device_id=(device_at(ORDERS[group][stage], towards),),
            device_id_type=MESH,
        )
        copy.start()
        flights[group, stage, kind] = copy
        sends.append(copy)

    def first_wave(group, stage):
        if stage == 0:
            arrive(group, 2)
        start(group, stage, 0, 2, 0, 1, 0)
        start(group, stage, 1, 2, 1, 3, 0)
        if stage == 0:
            arrive(group, 1)
        start(group, stage, 2, 1, 1, 1, 1)
        if stage == 0:
            arrive(group, 3)
        start(group, stage, 3, 3, 0, 3, 2)

    def second_wave(group, stage):
        buffer = bufs[(group * 3 + stage) * 3]
        for kind, part, step in ((0, 0, 1), (1, 1, 3)):
            flights[group, stage, kind].wait_recv()
            at, inner = window(group, fixed_at(group, stage, step), part)
            add(mine.at[at], buffer.at[inner])
            start(group, stage, 4 + kind, step, part, step, 1 + kind)

    def third_wave(group, stage):
        for kind in (2, 3, 4, 5):
            flights[group, stage, kind].wait_recv()
        at, _ = window(group, fixed_at(group, stage, 0), None)
        _, plus, minus = bufs[(group * 3 + stage) * 3 : (group * 3 + stage) * 3 + 3]
        if stage < 2:
            add(mine.at[at], plus, minus)
        else:
            first, length = GROUPS[group]
            out_ref[pl.ds(first, length), :] = mine[at] + plus[...] + minus[...]

    for groups in SETS:
        for group in groups:
            first_wave(group, 0)
    for stage in range(3):
        for groups in SETS:
            for group in groups:
                second_wave(group, stage)
        for groups in SETS:
            for group in groups:
                if stage == 0:
                    arrive(group, 0)
                third_wave(group, stage)
                if stage < 2:
                    first_wave(group, stage + 1)
    for copy in sends:
        copy.wait_send()


def reduce_scatter(acc):
    return pl.pallas_call(
        reduce_kernel,
        out_shape=jax.ShapeDtypeStruct((OWNER_ROWS, LANES), jnp.float32),
        in_specs=[pl.BlockSpec(memory_space=pltpu.VMEM)],
        out_specs=pl.BlockSpec(memory_space=pltpu.VMEM),
        scratch_shapes=[
            pltpu.VMEM((RING, RING, RING, OWNER_ROWS, LANES), jnp.float32),
            *ring_shapes(),
            pltpu.SemaphoreType.DMA((RING * len(GROUPS),)),
            pltpu.SemaphoreType.DMA((RING * len(GROUPS),)),
            pltpu.SemaphoreType.DMA((18 * len(GROUPS),)),
            pltpu.SemaphoreType.DMA((18 * len(GROUPS),)),
        ],
        compiler_params=pltpu.CompilerParams(collective_id=0, has_side_effects=True, vmem_limit_bytes=24 * 2**20),
        name="reduce_scatter",
    )(acc.reshape(RING, RING, RING, 2, OWNER_ROWS, LANES))


def body(a_blocks, p_blocks, a_slot, serve_rows, row_count, contrib_slot, recv_tile):
    me = lax.axis_index("elem")
    every = jnp.arange(N, dtype=jnp.int32)
    raw = p_blocks.reshape(R, KP, TILE_ROWS, LANES).transpose(0, 2, 1, 3).reshape(R, B, LANES)
    rows, outgoing = pl.pallas_call(
        serve_kernel,
        grid_spec=pltpu.PrefetchScalarGridSpec(
            num_scalar_prefetch=1,
            in_specs=[pl.BlockSpec(memory_space=pltpu.VMEM)],
            out_specs=(pl.BlockSpec(memory_space=pltpu.VMEM), pl.BlockSpec(memory_space=pltpu.HBM)),
            scratch_shapes=[pltpu.SemaphoreType.DMA],
        ),
        out_shape=(
            pltpu.VMEM((R, B, LANES), jnp.float32),
            pltpu.HBM((N * S, B, LANES), jnp.float32),
        ),
        compiler_params=pltpu.CompilerParams(vmem_limit_bytes=8 * 2**20),
        name="serve",
    )(serve_rows[0].T, raw)
    arrived = lax.all_to_all(outgoing, "elem", split_axis=0, concat_axis=0, tiled=True)

    mine = jnp.pad(recv_tile[0], ((0, 0), (0, LANES - CAP))).reshape(N, 1, LANES)
    told = pl.pallas_call(
        table_kernel,
        out_shape=jax.ShapeDtypeStruct((N, 1, LANES), jnp.int32),
        in_specs=[pl.BlockSpec(memory_space=pltpu.VMEM)],
        out_specs=pl.BlockSpec(memory_space=pltpu.VMEM),
        scratch_shapes=[pltpu.SemaphoreType.DMA] * 3,
        compiler_params=pltpu.CompilerParams(collective_id=1, has_side_effects=True, vmem_limit_bytes=4 * 2**20),
        cost_estimate=pl.CostEstimate(flops=0, bytes_accessed=2**20, transcendentals=0),
        name="table",
    )(mine)
    owner = lax.rem(me + every, N)
    table = (told[:, 0, :CAP] + owner[:, None] * TO).reshape(N * CAP)

    left = pl.pallas_call(
        left_kernel,
        grid_spec=pltpu.PrefetchScalarGridSpec(
            num_scalar_prefetch=1,
            grid=(R,),
            in_specs=[
                pl.BlockSpec(memory_space=pltpu.VMEM),
                pl.BlockSpec((1, KA, B, B), lambda i, c: (i, 0, 0, 0)),
            ],
            out_specs=pl.BlockSpec((1, KA, KP * B, LANES), lambda i, c: (i, 0, 0, 0), memory_space=pltpu.VMEM),
        ),
        out_shape=pltpu.HBM((R, KA, KP * B, LANES), jnp.bfloat16),
        compiler_params=pltpu.CompilerParams(vmem_limit_bytes=48 * 2**20),
        cost_estimate=pl.CostEstimate(flops=4 * 2 * R * KA * 128 * 64 * 64, bytes_accessed=16 * 2**20, transcendentals=0),
        name="left_products",
    )(row_count, rows, a_blocks.reshape(R, KA, B, B))

    slot = a_slot.reshape(R * KA)
    source = lax.rem(me + (2 * N - 1) - (slot - R) // S, N)
    ext_index = jnp.where(slot < R, slot, R + source * S + (slot - R) % S)
    acc = pl.pallas_call(
        tile_kernel,
        grid_spec=pltpu.PrefetchScalarGridSpec(
            num_scalar_prefetch=3,
            in_specs=[
                pl.BlockSpec(memory_space=pltpu.HBM),
                pl.BlockSpec(memory_space=pltpu.VMEM),
                pl.BlockSpec(memory_space=pltpu.HBM),
            ],
            out_specs=pl.BlockSpec(memory_space=pltpu.VMEM),
            scratch_shapes=[
                pltpu.VMEM((EXT, B, LANES), jnp.float32),
                pltpu.VMEM((R, KA, KP * B, LANES), jnp.bfloat16),
                pltpu.SemaphoreType.DMA((2,)),
                pltpu.SemaphoreType.DMA((PARTS,)),
            ],
        ),
        out_shape=pltpu.VMEM((N * TO, TILE_ROWS, LANES), jnp.float32),
        compiler_params=pltpu.CompilerParams(vmem_limit_bytes=42 * 2**20),
        cost_estimate=pl.CostEstimate(flops=4 * 2 * R * KA * 128 * 64 * 128, bytes_accessed=34 * 2**20, transcendentals=0),
        name="tiles",
    )(ext_index, contrib_slot.reshape(-1), table, left, rows, arrived)

    tiles = reduce_scatter(acc)
    return tiles.reshape(TO, TILE_ROWS, 2, B).transpose(0, 2, 1, 3).reshape(TO, B * B)


def solution(mesh):
    in_specs = (
        P("elem", None, None),
        P("elem", None, None),
        P("elem", None),
        P("elem", None, None),
        P("elem"),
        P("elem", None),
        P("elem", None, None),
    )

    return jax.shard_map(body, mesh=mesh, in_specs=in_specs, out_specs=P("elem", None), check_vma=False)
```

time: 225 us -> 236 us (1.049)
  Pallas kernels: 110 us -> 201 us
  waiting for transfers between devices: 59.4 us -> 0.01 us
  local copies, waits for them, and re-layouts: 30.1 us -> 18.9 us
  starting transfers between devices: 21.7 us -> 12.1 us
    pallas_call x0 -> x1, Pallas kernels: none -> 104 us  [body(): pl.pallas_call(table_kernel, out_shape=jax.ShapeDtypeStruct((N, 1, LANES)...]
    all_to_all x1, waiting for transfers between devices: 59.4 us -> 0.01 us  [body(): lax.all_to_all(outgoing, 'elem', split_axis=0, concat_axis=0, tiled=True)]
    all_to_all x1 -> x0, starting transfers between devices: 11.5 us -> none  [body(): told = lax.all_to_all(back, 'elem', split_axis=0, concat_axis=0, tiled=True)]
    reshape x5 -> x0, local copies, waits for them, and re-layouts: 9.45 us -> none  [the longest x3 8.62 us: body(): p_blocks.reshape(R, KP, B, B).transpose(0, 2, 1, 3).reshape(R, B, LANES)]
    pallas_call x1, Pallas kernels: 55.4 us -> 48.3 us  [reduce_scatter(): pl.pallas_call(reduce_kernel, out_shape=jax.ShapeDtypeStruct((OWNER_ROWS,...]
    pallas_call x1, Pallas kernels: 23 us -> 18.6 us  [body(): pl.pallas_call(tile_kernel, grid_spec=pltpu.PrefetchScalarGridSpec(num_sc...]
  transfers between devices with their start and end apart: 2 -> 1, of which waited for: 1 -> 0; matrix products, arithmetic and copies ran while one was open for 11% -> 7% of each run, Pallas kernels for 14% -> 55%
where the time goes in v2:
time: 236 us; the launch traced here: 234 us
  Pallas kernels  201 us (85%)
  local copies, waits for them, and re-layouts  18.9 us (8%)
  starting transfers between devices  12.1 us (5%)
    pallas_call x1, Pallas kernels, body(): pl.pallas_call(table_kernel, out_shape=jax.ShapeDtypeStruct((N, 1, LANES)...  104 us
    pallas_call x1, Pallas kernels, reduce_scatter(): pl.pallas_call(reduce_kernel, out_shape=jax.ShapeDtypeStruct((OWNER_ROWS,...  48.3 us
    pallas_call x1, Pallas kernels, body(): pl.pallas_call(left_kernel, grid_spec=pltpu.PrefetchScalarGridSpec(num_sc...  25.7 us
    pallas_call x1, Pallas kernels, body(): pl.pallas_call(tile_kernel, grid_spec=pltpu.PrefetchScalarGridSpec(num_sc...  18.6 us
    reshape x2, local copies, waits for them, and re-layouts, body(): a_blocks.reshape(R, KA, B, B)  14.5 us
    all_to_all x1, starting transfers between devices, body(): lax.all_to_all(outgoing, 'elem', split_axis=0, concat_axis=0, tiled=True)  12.1 us
  transfers between devices with their start and end apart: 1, of which 0 were waited for; matrix products, arithmetic and copies ran while one was open for 7% of the time, Pallas kernels for 55%

profile of v2, /device:TPU:1, one launch (start us, length us, event | category | flops | bytes accessed | tf_op | source)
XLA Modules:
  0.0 234.2 jit_solution(4506386403002794033)
XLA Ops:
  0.0 1.2 copy-done.1
  1.2 0.7 copy-done.2
  1.9 4.6 %serve.1 = (f32[32,64,128]{2,1,0:T(8,128)S(1)}, f32[256,64,128]{2,1,0:T(8,128)}) custom-call(s32[2,127]{1,0:T(2,128)S(1)} %bitcast.19, f32[32,64,128]{2,1,0:T(8,128)S(1)} %bitcast.17), custom_call_target="tpu_custom_call" | custom-call | tf_op jit(solution)/shard_map/serve/pallas_call | solution.py:342
  6.6 0.0 copy-start.4
  6.6 0.0 copy-start.5
  6.6 12.1 %all-to-all-start = ((f32[256,64,128]{2,1,0:T(8,128)}), f32[256,64,128]{2,1,0:T(8,128)}, u32[]{:S(2)}, u32[]{:S(2)}) async-start(f32[256,64,128]{2,1,0:T(8,128)} %get-tuple-element.8), calls=%async_computation | async-start | bytes 16777216 | tf_op jit(solution)/shard_map/all_to_all | solution.py:357
  19.3 0.7 reshape.43.slot_ref
  20.0 0.1 copy.12
  20.1 0.1 reshape.42
  20.2 0.1 add.46
  20.3 0.1 add.47
  20.4 0.1 copy.13
  20.5 104.0 %table.1 = s32[128,1,128]{2,1,0:T(1,128)S(1)} custom-call(s32[128,1,128]{2,1,0:T(1,128)S(1)} %bitcast.18), custom_call_target="tpu_custom_call" | custom-call | bytes 1048576 | tf_op jit(solution)/shard_map/table/pallas_call | solution.py:360
  124.5 0.2 slice_reduce_fusion
  124.7 0.1 squeeze.10
  124.8 7.0 %reshape.47 = f32[32,7,64,64]{3,2,0,1:T(8,128)} reshape(f32[32,7,4096]{2,0,1:T(8,128)} %param.7) | data formatting | bytes 7340032 | tf_op jit(solution)/shard_map/reshape | solution.py:388
  131.9 7.5 %copy.15.a_ref = f32[32,7,64,64]{3,2,1,0:T(8,128)} copy(f32[32,7,64,64]{3,2,0,1:T(8,128)} %reshape.47) | data formatting | bytes 7340032 | tf_op jit(solution)/shard_map/reshape | solution.py:388
  139.3 0.6 add.48.table_ref
  139.9 25.7 %left_products.1.left_ref = bf16[32,7,128,128]{3,2,1,0:T(8,128)(2,1)} custom-call(s32[1]{0:T(128)S(6)} %copy.17.count_ref, f32[32,64,128]{2,1,0:T(8,128)S(1)} %get-tuple-element.7.p_ref.own_ref, f32[32,7,64,64]{3,2,1,0:T(8,128)} %copy.15.a_ref), custom_call_target="tpu_custom_call" | custom-call | flops 939524096 | bytes 16777216 | tf_op jit(solution)/shard_map/left_products/pallas_call | solution.py:373
  165.7 0.6 compare_select_fusion.index_ref
  166.3 18.6 %tiles.1 = f32[1024,32,128]{2,1,0:T(8,128)S(1)} custom-call(s32[224]{0:T(256)} %compare_select_fusion.index_ref, s32[896]{0:T(1024)} %reshape.43.slot_ref, s32[512]{0:T(512)} %add.48.table_ref, bf16[32,7,128,128]{3,2,1,0:T(8,128)(2,1)} %left_products.1.left_ref, f32[32,64,128]{2,1,0:T(8,128)} %copy-done, f32[256,64,128]{2,1,0:T(8,128)} %all-to-all-done.far_ref), custom_call_target="tpu_custom_call" | custom-call | flops 1879048192 | bytes 35651584 | tf_op jit(solution)/shard_map/tiles/pallas_call | solution.py:393
  184.9 48.3 %reduce_scatter.1 = f32[256,128]{1,0:T(8,128)S(1)} custom-call(f32[4,4,4,2,256,128]{5,4,3,2,1,0:T(8,128)S(1)} %bitcast.16), custom_call_target="tpu_custom_call" | custom-call | tf_op jit(solution)/shard_map/reduce_scatter/pallas_call | solution.py:320
  233.2 0.2 reshape.49
  233.4 0.8 reshape.50
  (12 shorter events, 0.1 us)
Async XLA Ops:
  0.0 1.2 copy-start.1
  1.2 0.7 copy-start.2
  6.5 133.4 %copy-start = (f32[32,64,128]{2,1,0:T(8,128)}, f32[32,64,128]{2,1,0:T(8,128)S(1)}, u32[]{:S(2)}) copy-start(f32[32,64,128]{2,1,0:T(8,128)S(1)} %get-tuple-element.7.p_ref.own_ref) | copy-start | bytes 3145732
  6.5 12.8 %copy-start.3 = (s32[32,28]{1,0:T(8,128)S(1)}, s32[32,28]{1,0:T(8,128)}, u32[]{:S(2)}) copy-start(s32[32,28]{1,0:T(8,128)} %param.12) | copy-start | bytes 10756
  6.6 13.4 %copy-start.4 = (s32[32,7]{0,1:T(8,128)S(1)}, s32[32,7]{0,1:T(8,128)}, u32[]{:S(2)}) copy-start(s32[32,7]{0,1:T(8,128)} %param.9) | copy-start | bytes 2692
  6.6 13.8 %copy-start.5 = (s32[1,128,4]{1,2,0:T(4,128)S(1)}, s32[1,128,4]{1,2,0:T(4,128)}, u32[]{:S(2)}) copy-start(s32[1,128,4]{1,2,0:T(4,128)} %param.13) | copy-start | bytes 6148
  6.6 159.7 %all-to-all-start = ((f32[256,64,128]{2,1,0:T(8,128)}), f32[256,64,128]{2,1,0:T(8,128)}, u32[]{:S(2)}, u32[]{:S(2)}) async-start(f32[256,64,128]{2,1,0:T(8,128)} %get-tuple-element.8), calls=%async_computation | async-start | bytes 16777216 | tf_op jit(solution)/shard_map/all_to_all | solution.py:357

commit v3 on v2

--- a/solution.py
+++ b/solution.py
@@ -53,7 +53,7 @@
     pltpu.make_async_copy(out_ref, out_ref, sem).wait()
 
 
-def table_kernel(tiles_ref, out_ref, send_sem, recv_sem, own_sem):
+def table_kernel(tiles_ref, after_ref, out_ref, send_sem, recv_sem, own_sem):
     me = lax.axis_index("elem")
 
     def greet(m, carry):
@@ -194,7 +194,7 @@
         return ((at[0] * RING + at[1]) * RING + at[2]) * 2 + core
 
     barrier = pltpu.get_barrier_semaphore()
-    near = [partner] + [device_at(axis, step) for axis in range(3) for step in (1, 3)]
+    near = [partner] + [device_at(axis, step) for axis in range(3) for step in (1, 2, 3)]
     for other in near:
         pl.semaphore_signal(barrier, inc=1, device_id=(other,), device_id_type=MESH)
     pl.semaphore_wait(barrier, len(near))
@@ -267,17 +267,25 @@
         flights[group, stage, kind] = copy
         sends.append(copy)
 
-    def first_wave(group, stage):
-        if stage == 0:
-            arrive(group, 2)
-        start(group, stage, 0, 2, 0, 1, 0)
-        start(group, stage, 1, 2, 1, 3, 0)
-        if stage == 0:
-            arrive(group, 1)
-        start(group, stage, 2, 1, 1, 1, 1)
-        if stage == 0:
-            arrive(group, 3)
-        start(group, stage, 3, 3, 0, 3, 2)
+    def first_wave(groups, stage):
+        for step, sends_of in ((2, ((0, 0, 1, 0), (1, 1, 3, 0))), (1, ((2, 1, 1, 1),)), (3, ((3, 0, 3, 2),))):
+            for group in groups:
+                if stage == 0:
+                    arrive(group, step)
+                for kind, part, towards, buffer in sends_of:
+                    start(group, stage, kind, step, part, towards, buffer)
+
+    def last_wave(groups):
+        for kind, step in ((1, 2), (0, 1), (2, 3)):
+            for group in groups:
+                start(group, 2, kind, step, None, step, kind)
+        for group in groups:
+            for kind in range(3):
+                flights[group, 2, kind].wait_recv()
+            at, _ = window(group, fixed_at(group, 2, 0), None)
+            first, length = GROUPS[group]
+            terms = bufs[(group * 3 + 2) * 3 : (group * 3 + 2) * 3 + 3]
+            out_ref[pl.ds(first, length), :] = mine[at] + terms[0][...] + terms[1][...] + terms[2][...]
 
     def second_wave(group, stage):
         buffer = bufs[(group * 3 + stage) * 3]
@@ -292,16 +300,11 @@
             flights[group, stage, kind].wait_recv()
         at, _ = window(group, fixed_at(group, stage, 0), None)
         _, plus, minus = bufs[(group * 3 + stage) * 3 : (group * 3 + stage) * 3 + 3]
-        if stage < 2:
-            add(mine.at[at], plus, minus)
-        else:
-            first, length = GROUPS[group]
-            out_ref[pl.ds(first, length), :] = mine[at] + plus[...] + minus[...]
+        add(mine.at[at], plus, minus)
 
     for groups in SETS:
-        for group in groups:
-            first_wave(group, 0)
-    for stage in range(3):
+        first_wave(groups, 0)
+    for stage in range(2):
         for groups in SETS:
             for group in groups:
                 second_wave(group, stage)
@@ -310,8 +313,10 @@
                 if stage == 0:
                     arrive(group, 0)
                 third_wave(group, stage)
-                if stage < 2:
-                    first_wave(group, stage + 1)
+            if stage == 0:
+                first_wave(groups, 1)
+    for groups in SETS:
+        last_wave(groups)
     for copy in sends:
         copy.wait_send()
 
@@ -356,20 +361,6 @@
     )(serve_rows[0].T, raw)
     arrived = lax.all_to_all(outgoing, "elem", split_axis=0, concat_axis=0, tiled=True)
 
-    mine = jnp.pad(recv_tile[0], ((0, 0), (0, LANES - CAP))).reshape(N, 1, LANES)
-    told = pl.pallas_call(
-        table_kernel,
-        out_shape=jax.ShapeDtypeStruct((N, 1, LANES), jnp.int32),
-        in_specs=[pl.BlockSpec(memory_space=pltpu.VMEM)],
-        out_specs=pl.BlockSpec(memory_space=pltpu.VMEM),
-        scratch_shapes=[pltpu.SemaphoreType.DMA] * 3,
-        compiler_params=pltpu.CompilerParams(collective_id=1, has_side_effects=True, vmem_limit_bytes=4 * 2**20),
-        cost_estimate=pl.CostEstimate(flops=0, bytes_accessed=2**20, transcendentals=0),
-        name="table",
-    )(mine)
-    owner = lax.rem(me + every, N)
-    table = (told[:, 0, :CAP] + owner[:, None] * TO).reshape(N * CAP)
-
     left = pl.pallas_call(
         left_kernel,
         grid_spec=pltpu.PrefetchScalarGridSpec(
@@ -386,6 +377,20 @@
         cost_estimate=pl.CostEstimate(flops=4 * 2 * R * KA * 128 * 64 * 64, bytes_accessed=16 * 2**20, transcendentals=0),
         name="left_products",
     )(row_count, rows, a_blocks.reshape(R, KA, B, B))
+
+    mine = jnp.pad(recv_tile[0], ((0, 0), (0, LANES - CAP))).reshape(N, 1, LANES)
+    told = pl.pallas_call(
+        table_kernel,
+        out_shape=jax.ShapeDtypeStruct((N, 1, LANES), jnp.int32),
+        in_specs=[pl.BlockSpec(memory_space=pltpu.VMEM), pl.BlockSpec(memory_space=pltpu.HBM)],
+        out_specs=pl.BlockSpec(memory_space=pltpu.VMEM),
+        scratch_shapes=[pltpu.SemaphoreType.DMA] * 3,
+        compiler_params=pltpu.CompilerParams(collective_id=1, has_side_effects=True, vmem_limit_bytes=58 * 2**20),
+        cost_estimate=pl.CostEstimate(flops=0, bytes_accessed=2**20, transcendentals=0),
+        name="table",
+    )(mine, left)
+    owner = lax.rem(me + every, N)
+    table = (told[:, 0, :CAP] + owner[:, None] * TO).reshape(N * CAP)
 
     slot = a_slot.reshape(R * KA)
     source = lax.rem(me + (2 * N - 1) - (slot - R) // S, N)

time: 236 us -> 198 us (0.84)
  Pallas kernels: 201 us -> 161 us
    pallas_call x1, Pallas kernels: 104 us -> 63.7 us  [body(): pl.pallas_call(table_kernel, out_shape=jax.ShapeDtypeStruct((N, 1, LANES)...]
  transfers between devices with their start and end apart: 1 -> 1, of which waited for: 0 -> 0; matrix products, arithmetic and copies ran while one was open for 7% -> 10% of each run, Pallas kernels for 55% -> 46%
where the time goes in v3:
time: 198 us; the launch traced here: 196 us
  Pallas kernels  161 us (81%)
  local copies, waits for them, and re-layouts  20.4 us (10%)
  starting transfers between devices  12.1 us (6%)
    pallas_call x1, Pallas kernels, body(): pl.pallas_call(table_kernel, out_shape=jax.ShapeDtypeStruct((N, 1, LANES)...  63.7 us
    pallas_call x1, Pallas kernels, reduce_scatter(): pl.pallas_call(reduce_kernel, out_shape=jax.ShapeDtypeStruct((OWNER_ROWS,...  48.6 us
    pallas_call x1, Pallas kernels, body(): pl.pallas_call(left_kernel, grid_spec=pltpu.PrefetchScalarGridSpec(num_sc...  25.7 us
    pallas_call x1, Pallas kernels, body(): pl.pallas_call(tile_kernel, grid_spec=pltpu.PrefetchScalarGridSpec(num_sc...  18.6 us
    reshape x2, local copies, waits for them, and re-layouts, body(): a_blocks.reshape(R, KA, B, B)  14.5 us
    all_to_all x1, starting transfers between devices, body(): lax.all_to_all(outgoing, 'elem', split_axis=0, concat_axis=0, tiled=True)  12.1 us
    pallas_call x1, Pallas kernels, body(): pl.pallas_call(serve_kernel, grid_spec=pltpu.PrefetchScalarGridSpec(num_s...  4.62 us
  transfers between devices with their start and end apart: 1, of which 0 were waited for; matrix products, arithmetic and copies ran while one was open for 10% of the time, Pallas kernels for 46%

profile of v3, /device:TPU:1, one launch (start us, length us, event | category | flops | bytes accessed | tf_op | source)
XLA Modules:
  0.0 195.6 jit_solution(14085272851901731604)
XLA Ops:
  0.0 1.2 copy-done.1
  1.2 0.7 copy-done.2
  1.9 4.6 %serve.1 = (f32[32,64,128]{2,1,0:T(8,128)S(1)}, f32[256,64,128]{2,1,0:T(8,128)}) custom-call(s32[2,127]{1,0:T(2,128)S(1)} %bitcast.18, f32[32,64,128]{2,1,0:T(8,128)S(1)} %bitcast.17), custom_call_target="tpu_custom_call" | custom-call | tf_op jit(solution)/shard_map/serve/pallas_call | solution.py:347
  6.6 0.0 copy-start.4
  6.6 12.1 %all-to-all-start = ((f32[256,64,128]{2,1,0:T(8,128)}), f32[256,64,128]{2,1,0:T(8,128)}, u32[]{:S(2)}, u32[]{:S(2)}) async-start(f32[256,64,128]{2,1,0:T(8,128)} %get-tuple-element.8), calls=%async_computation | async-start | bytes 16777216 | tf_op jit(solution)/shard_map/all_to_all | solution.py:362
  19.3 0.7 reshape.43.slot_ref
  20.0 0.1 copy.12
  20.1 0.1 reshape.42
  20.2 0.1 add.46
  20.3 0.1 add.47
  20.4 0.1 copy.13
  20.5 7.0 %reshape.47 = f32[32,7,64,64]{3,2,0,1:T(8,128)} reshape(f32[32,7,4096]{2,0,1:T(8,128)} %param.7) | data formatting | bytes 7340032 | tf_op jit(solution)/shard_map/reshape | solution.py:379
  27.6 7.5 %copy.15.a_ref = f32[32,7,64,64]{3,2,1,0:T(8,128)} copy(f32[32,7,64,64]{3,2,0,1:T(8,128)} %reshape.47) | data formatting | bytes 7340032 | tf_op jit(solution)/shard_map/reshape | solution.py:379
  35.1 0.6 pad.4
  35.7 25.7 %left_products.1.after_ref.left_ref = bf16[32,7,128,128]{3,2,1,0:T(8,128)(2,1)} custom-call(s32[1]{0:T(128)S(6)} %copy.17.count_ref, f32[32,64,128]{2,1,0:T(8,128)S(1)} %get-tuple-element.7.p_ref.own_ref, f32[32,7,64,64]{3,2,1,0:T(8,128)} %copy.15.a_ref), custom_call_target="tpu_custom_call" | custom-call | flops 939524096 | bytes 16777216 | tf_op jit(solution)/shard_map/left_products/pallas_call | solution.py:364
  61.4 63.7 %table.1 = s32[128,1,128]{2,1,0:T(1,128)} custom-call(s32[128,1,128]{2,1,0:T(1,128)} %bitcast.20, bf16[32,7,128,128]{3,2,1,0:T(8,128)(2,1)} %left_products.1.after_ref.left_ref), custom_call_target="tpu_custom_call" | custom-call | bytes 1048576 | tf_op jit(solution)/shard_map/table/pallas_call | solution.py:382
  125.1 1.0 slice_reduce_fusion
  126.1 0.1 squeeze.11
  126.2 0.6 add.48.table_ref
  126.8 0.6 compare_select_fusion.index_ref
  127.4 18.6 %tiles.1 = f32[1024,32,128]{2,1,0:T(8,128)S(1)} custom-call(s32[224]{0:T(256)} %compare_select_fusion.index_ref, s32[896]{0:T(1024)} %reshape.43.slot_ref, s32[512]{0:T(512)} %add.48.table_ref, bf16[32,7,128,128]{3,2,1,0:T(8,128)(2,1)} %left_products.1.after_ref.left_ref, f32[32,64,128]{2,1,0:T(8,128)} %copy-done, f32[256,64,128]{2,1,0:T(8,128)} %all-to-all-done.far_ref), custom_call_target="tpu_custom_call" | custom-call | flops 1879048192 | bytes 35651584 | tf_op jit(solution)/shard_map/tiles/pallas_call | solution.py:398
  146.0 48.6 %reduce_scatter.1 = f32[256,128]{1,0:T(8,128)S(1)} custom-call(f32[4,4,4,2,256,128]{5,4,3,2,1,0:T(8,128)S(1)} %bitcast.16), custom_call_target="tpu_custom_call" | custom-call | tf_op jit(solution)/shard_map/reduce_scatter/pallas_call | solution.py:325
  194.6 0.2 reshape.49
  194.9 0.8 reshape.50
  (12 shorter events, 0.1 us)
Async XLA Ops:
  0.0 1.2 copy-start.1
  1.2 0.7 copy-start.2
  6.5 29.2 %copy-start = (f32[32,64,128]{2,1,0:T(8,128)}, f32[32,64,128]{2,1,0:T(8,128)S(1)}, u32[]{:S(2)}) copy-start(f32[32,64,128]{2,1,0:T(8,128)S(1)} %get-tuple-element.7.p_ref.own_ref) | copy-start | bytes 3145732
  6.5 12.8 %copy-start.3 = (s32[32,28]{1,0:T(8,128)S(1)}, s32[32,28]{1,0:T(8,128)}, u32[]{:S(2)}) copy-start(s32[32,28]{1,0:T(8,128)} %param.12) | copy-start | bytes 10756
  6.6 13.4 %copy-start.4 = (s32[32,7]{0,1:T(8,128)S(1)}, s32[32,7]{0,1:T(8,128)}, u32[]{:S(2)}) copy-start(s32[32,7]{0,1:T(8,128)} %param.9) | copy-start | bytes 2692
  6.6 13.8 %copy-start.5 = (s32[1,128,4]{1,2,0:T(4,128)S(1)}, s32[1,128,4]{1,2,0:T(4,128)}, u32[]{:S(2)}) copy-start(s32[1,128,4]{1,2,0:T(4,128)} %param.13) | copy-start | bytes 6148
  6.6 120.8 %all-to-all-start = ((f32[256,64,128]{2,1,0:T(8,128)}), f32[256,64,128]{2,1,0:T(8,128)}, u32[]{:S(2)}, u32[]{:S(2)}) async-start(f32[256,64,128]{2,1,0:T(8,128)} %get-tuple-element.8), calls=%async_computation | async-start | bytes 16777216 | tf_op jit(solution)/shard_map/all_to_all | solution.py:362

commit v4 on v3

--- a/solution.py
+++ b/solution.py
@@ -18,8 +18,6 @@
 LANES = 128
 TILE_ROWS = B * B // LANES
 OWNER_ROWS = TO * TILE_ROWS
-EXT = R + N * S
-PARTS = 4
 MESH = pl.DeviceIdType.MESH
 
 GROUPS = ((0, 40), (40, 48), (88, 40), (128, 48), (176, 40), (216, 40))
@@ -27,8 +25,47 @@
 SETS = ((0, 1, 2), (3, 4, 5))
 
 
-def serve_kernel(serve_ref, raw_ref, rows_ref, out_ref, sem):
+def split(value):
+    high = value.astype(jnp.bfloat16)
+    low = (value - high.astype(jnp.float32)).astype(jnp.bfloat16)
+    return high, low
+
+
+LINES = ((0, 24), (24, 24), (48, 16), (64, 16), (80, 24), (104, 24))
+SHARES = (8, 8, 6, 6, 4)
+
+
+def relay_shapes():
+    return [pltpu.VMEM((RING, RING, length, LANES), jnp.float32) for _, length in LINES for _ in range(6)]
+
+
+def exchange_kernel(serve_ref, count_ref, raw_ref, tiles_ref, a_hbm, rows_ref, far_ref, left_ref, told_ref, *rest):
+    out, first_hop, second_hop, a_ref = rest[:4]
+    relays = rest[4:40]
+    send, recv, local, a_sem, told_send, told_recv, told_own = rest[40:]
+    hops = (out, first_hop, second_hop, far_ref)
     me = lax.axis_index("elem")
+    core = me % 2
+    chip = me // 2
+    place = (chip // (RING * RING), (chip // RING) % RING, chip % RING)
+
+    def device_at(axis, step, core_at):
+        at = list(place)
+        at[axis] = (at[axis] + step) % RING
+        return ((at[0] * RING + at[1]) * RING + at[2]) * 2 + core_at
+
+    barrier = pltpu.get_barrier_semaphore()
+
+    def greet(m, carry):
+        pl.semaphore_signal(barrier, inc=1, device_id=(lax.rem(me + m, N),), device_id_type=MESH)
+        return carry
+
+    lax.fori_loop(1, N, greet, 0)
+    a_copy = pltpu.make_async_copy(a_hbm, a_ref, a_sem)
+    a_copy.start()
+    own_tiles = pltpu.make_async_copy(tiles_ref.at[0], told_ref.at[0], told_own)
+    own_tiles.start()
+
     lane = lax.broadcasted_iota(jnp.int32, (B, LANES), 1) < B
     even = lax.broadcasted_iota(jnp.int32, (B, LANES), 0) % 2 == 0
 
@@ -39,96 +76,192 @@
         rows_ref[n] = jnp.where(lane == even, raw, other)
         return carry
 
-    lax.fori_loop(0, R, turn, 0, unroll=4)
-
-    def send(n, carry):
-        to = lax.rem(me + 1 + n, N)
+    lax.fori_loop(0, R, turn, 0)
+
+    def place_of(device):
+        return device // (2 * RING * RING), (device // (2 * RING)) % RING, (device // 2) % RING, device % 2
+
+    def gather(n, carry):
+        y, x, z, k = place_of(lax.rem(me + 1 + n, N))
         for c in range(S):
-            pltpu.make_async_copy(rows_ref.at[serve_ref[c, n]], out_ref.at[to * S + c], sem).start()
-        return carry
-
-    lax.fori_loop(0, N - 1, send, 0)
-    for c in range(S):
-        pltpu.make_async_copy(rows_ref.at[0], out_ref.at[me * S + c], sem).start()
-    pltpu.make_async_copy(out_ref, out_ref, sem).wait()
-
-
-def table_kernel(tiles_ref, after_ref, out_ref, send_sem, recv_sem, own_sem):
-    me = lax.axis_index("elem")
-
-    def greet(m, carry):
-        pl.semaphore_signal(barrier, inc=1, device_id=(lax.rem(me + m, N),), device_id_type=MESH)
-        return carry
-
-    def send(m, carry):
+            out[y, x, z, k, c * B : (c + 1) * B, :] = rows_ref[serve_ref[c, n]]
+        return carry
+
+    lax.fori_loop(0, N - 1, gather, 0)
+    out[place[0], place[1], place[2], core] = jnp.zeros((S * B, LANES), jnp.float32)
+    pl.semaphore_wait(barrier, N - 1)
+
+    def tell(m, carry):
         pltpu.make_async_remote_copy(
             src_ref=tiles_ref.at[m],
-            dst_ref=out_ref.at[m],
-            send_sem=send_sem,
-            recv_sem=recv_sem,
+            dst_ref=told_ref.at[m],
+            send_sem=told_send,
+            recv_sem=told_recv,
             device_id=(lax.rem(me + N - m, N),),
             device_id_type=MESH,
         ).start()
         return carry
 
-    own = pltpu.make_async_copy(tiles_ref.at[0], out_ref.at[0], own_sem)
-    own.start()
-    barrier = pltpu.get_barrier_semaphore()
-    lax.fori_loop(1, N, greet, 0)
-    pl.semaphore_wait(barrier, N - 1)
-    lax.fori_loop(1, N, send, 0)
-    own.wait()
-    rest = pl.ds(1, N - 1)
-    pltpu.make_async_copy(tiles_ref.at[rest], tiles_ref.at[rest], send_sem).wait()
-    pltpu.make_async_copy(out_ref.at[rest], out_ref.at[rest], recv_sem).wait()
-
-
-def split(value):
-    high = value.astype(jnp.bfloat16)
-    low = (value - high.astype(jnp.float32)).astype(jnp.bfloat16)
-    return high, low
-
-
-def left_kernel(count_ref, p_ref, a_ref, out_ref):
-    row = pl.program_id(0)
-    high, low = split(p_ref[row].T)
-    left = jnp.concatenate([high, low], axis=1)
-    lane = lax.broadcasted_iota(jnp.int32, (KP * B, LANES), 1)
-    for k in range(KA):
-        a_high, a_low = split(a_ref[0, k])
-        wide = jnp.concatenate([a_high, a_low], axis=1)
-        both = jnp.dot(left, jnp.concatenate([wide, wide], axis=0), preferred_element_type=jnp.float32)
-        twice = both + pltpu.roll(both, B, 1)
-        twice = jnp.where(row < count_ref[0], twice, 0.0)
-        m_high = twice.astype(jnp.bfloat16).astype(jnp.float32)
-        out_ref[0, k] = jnp.where(lane < B, m_high, twice - m_high).astype(jnp.bfloat16)
-
-
-def tile_kernel(index_ref, slot_ref, table_ref, left_ref, own_ref, far_ref, acc, ext, m_ref, load_sem, left_sem):
-    own = pltpu.make_async_copy(own_ref, ext.at[pl.ds(0, R)], load_sem.at[0])
-    far = pltpu.make_async_copy(far_ref, ext.at[pl.ds(R, N * S)], load_sem.at[1])
-    far.start()
-    own.start()
-    parts = []
-    for n in range(PARTS):
-        some = pl.ds(n * (R // PARTS), R // PARTS)
-        parts.append(pltpu.make_async_copy(left_ref.at[some], m_ref.at[some], left_sem.at[n]))
-        parts[n].start()
+    lax.fori_loop(1, N, tell, 0)
+
+    def window(group, axis, at_axis, core_at):
+        at = [slice(None)] * 3
+        at[axis] = at_axis
+        return tuple(at) + (slice(None) if core_at is None else core_at, pl.ds(*LINES[group]), slice(None))
+
+    sent = []
+    arrivals = {}
+
+    def fly(group, phase, kind, source, target, device, lane_of=0):
+        base = (group * 3 + phase) * 9
+        copy = pltpu.make_async_remote_copy(
+            src_ref=source,
+            dst_ref=target,
+            send_sem=send.at[base + kind],
+            recv_sem=recv.at[base + lane_of],
+            device_id=(device,),
+            device_id_type=MESH,
+        )
+        copy.start()
+        sent.append(copy)
+
+    def land(group, phase, lane_of, like):
+        pltpu.make_async_copy(like, like, recv.at[(group * 3 + phase) * 9 + lane_of]).wait()
+
+    def first_wave(groups, phase):
+        source, target = hops[phase], hops[phase + 1]
+        for group in groups:
+            axis = ORDERS[group][phase]
+            u = place[axis]
+            for part, step in ((0, 1), (1, 3)):
+                relay = relays[(group * 3 + phase) * 2 + part]
+                src = source.at[window(group, axis, (u + 2) % RING, part)]
+                fly(group, phase, part, src, relay, device_at(axis, step, core), part)
+        for side, step in ((0, 1), (1, 3)):
+            for group in groups:
+                axis = ORDERS[group][phase]
+                u = place[axis]
+                to = (u + step) % RING
+                if phase < 2:
+                    at = window(group, axis, u, None)
+                    fly(group, phase, 2 + side, source.at[window(group, axis, to, None)], target.at[at], device_at(axis, step, core), 2 + side)
+                else:
+                    at = window(group, axis, u, core)
+                    for part in range(2):
+                        kind = 2 + 2 * side + part
+                        src = source.at[window(group, axis, to, part)]
+                        fly(group, phase, kind, src, target.at[at], device_at(axis, step, part), 2 + 2 * side + core)
+        for group in groups:
+            axis = ORDERS[group][phase]
+            u = place[axis]
+            at = window(group, axis, u, None if phase < 2 else core)
+            keep = pltpu.make_async_copy(source.at[at], target.at[at], local.at[group * 3 + phase])
+            keep.start()
+            arrivals[group, phase] = keep
+            if phase == 2:
+                src = source.at[window(group, axis, u, 1 - core)]
+                fly(group, phase, 8, src, target.at[at], device_at(axis, 0, 1 - core), 8)
+
+    def second_wave(groups, phase):
+        target = hops[phase + 1]
+        for group in groups:
+            axis = ORDERS[group][phase]
+            u = place[axis]
+            for part, step in ((0, 1), (1, 3)):
+                relay = relays[(group * 3 + phase) * 2 + part]
+                land(group, phase, part, relay)
+                origin = (u + RING - step) % RING
+                if phase < 2:
+                    at = window(group, axis, origin, part)
+                    fly(group, phase, 6 + part, relay, target.at[at], device_at(axis, step, core), 6 + part)
+                else:
+                    at = window(group, axis, origin, core)
+                    fly(group, phase, 6 + part, relay, target.at[at], device_at(axis, step, part), 6 + core)
+
+    def third_wave(groups, phase):
+        target = hops[phase + 1]
+        for group in groups:
+            axis = ORDERS[group][phase]
+            u = place[axis]
+            arrivals[group, phase].wait()
+            for side in range(2):
+                if phase < 2:
+                    land(group, phase, 2 + side, target.at[window(group, axis, u, None)])
+                else:
+                    land(group, phase, 2 + 2 * side, target.at[window(group, axis, u, core)])
+                    land(group, phase, 3 + 2 * side, target.at[window(group, axis, u, core)])
+            land(group, phase, 6, target.at[window(group, axis, u, core)])
+            land(group, phase, 7, target.at[window(group, axis, u, core)])
+            if phase == 2:
+                land(group, phase, 8, target.at[window(group, axis, u, core)])
+
+    def left_row(row, carry):
+        low_half = lax.broadcasted_iota(jnp.int32, (TILE_ROWS, LANES), 1) < B
+        stack = [rows_ref[row, pl.ds(h, TILE_ROWS, stride=2), :] for h in range(2)]
+        high, low = split(jnp.concatenate(stack, axis=0).T)
+        factor = jnp.concatenate([high, low], axis=1)
+        for k in range(KA):
+            block = a_ref[k * (R // 8) + row // 8, pl.ds(row % 8, TILE_ROWS, stride=8), :]
+            turned = pltpu.roll(block, B, 1)
+            value = jnp.concatenate([jnp.where(low_half, block, turned), jnp.where(low_half, turned, block)], axis=0)
+            top = value.astype(jnp.bfloat16).astype(jnp.float32)
+            wide = jnp.where(lane, top, value - top).astype(jnp.bfloat16)
+            both = jnp.dot(factor, jnp.concatenate([wide, wide], axis=0), preferred_element_type=jnp.float32)
+            twice = both + pltpu.roll(both, B, 1)
+            m_high = twice.astype(jnp.bfloat16).astype(jnp.float32)
+            wide_lane = lax.broadcasted_iota(jnp.int32, (KP * B, LANES), 1) < B
+            left_ref[row, k] = jnp.where(wide_lane, m_high, twice - m_high).astype(jnp.bfloat16)
+        return carry
+
+    def left_share(n):
+        done = sum(SHARES[:n])
+        lax.fori_loop(done, done + SHARES[n], left_row, 0)
+
+    for groups in SETS:
+        first_wave(groups, 0)
+    a_copy.wait()
+    left_share(0)
+    for phase in range(3):
+        for groups in SETS:
+            second_wave(groups, phase)
+        if phase < 2:
+            left_share(2 * phase + 1)
+        for groups in SETS:
+            third_wave(groups, phase)
+            if phase < 2:
+                first_wave(groups, phase + 1)
+        if phase < 2:
+            left_share(2 * phase + 2)
+    own_tiles.wait()
+    others = pl.ds(1, N - 1)
+    pltpu.make_async_copy(tiles_ref.at[others], tiles_ref.at[others], told_send).wait()
+    pltpu.make_async_copy(told_ref.at[others], told_ref.at[others], told_recv).wait()
+    for copy in sent:
+        copy.wait_send()
+
+
+def tile_kernel(count_ref, row_ref, slot_ref, left_ref, own_ref, far_ref, told_ref, acc, told, told_sem):
+    me = lax.axis_index("elem")
+    told_copy = pltpu.make_async_copy(told_ref, told, told_sem)
+    told_copy.start()
 
     def clear(n, carry):
         acc[pl.ds(n * 8, 8)] = jnp.zeros((8, TILE_ROWS, LANES), jnp.float32)
         return carry
 
     lax.fori_loop(0, N * TO // 8, clear, 0)
-    own.wait()
-    far.wait()
+    told_copy.wait()
     lane = lax.broadcasted_iota(jnp.int32, (TILE_ROWS, LANES), 1)
 
     def step(row, carry):
         for k in range(KA):
-            high, low = split(ext[index_ref[row * KA + k]])
+            index = row_ref[k, row]
+            away = jnp.maximum(index - R, 0)
+            own = own_ref[jnp.minimum(index, R - 1)]
+            far = far_ref[((me + 2 * N - 1 - away // S) % N) * S + away % S]
+            high, low = split(jnp.where(index < R, own, far))
             wide = jnp.concatenate([high, low], axis=1)
-            both = jnp.dot(m_ref[row, k], jnp.concatenate([wide, wide], axis=0), preferred_element_type=jnp.float32)
+            both = jnp.dot(left_ref[row, k], jnp.concatenate([wide, wide], axis=0), preferred_element_type=jnp.float32)
             part = both[:, :LANES] + both[:, LANES:]
             turned = pltpu.roll(part, B, 1)
             for p in range(KP):
@@ -137,13 +270,13 @@
                 upper_t, lower_t = turned[top : top + TILE_ROWS], turned[bottom : bottom + TILE_ROWS]
                 tiles = (jnp.where(lane < B, upper, lower_t), jnp.where(lane < B, upper_t, lower))
                 for q in range(KP):
-                    target = table_ref[slot_ref[row * (KP * KA * KP) + p * (KA * KP) + k * KP + q]]
+                    slot = slot_ref[row, p * (KA * KP) + k * KP + q]
+                    position = slot // CAP
+                    target = ((me + position) % N) * TO + told[position, 0, slot % CAP]
                     acc[target] += tiles[q]
         return carry
 
-    for n in range(PARTS):
-        parts[n].wait()
-        lax.fori_loop(n * (R // PARTS), (n + 1) * (R // PARTS), step, 0)
+    lax.fori_loop(0, jnp.minimum(count_ref[0], R), step, 0)
 
 
 def ring_shapes():
@@ -335,91 +468,57 @@
             pltpu.SemaphoreType.DMA((18 * len(GROUPS),)),
             pltpu.SemaphoreType.DMA((18 * len(GROUPS),)),
         ],
-        compiler_params=pltpu.CompilerParams(collective_id=0, has_side_effects=True, vmem_limit_bytes=24 * 2**20),
+        compiler_params=pltpu.CompilerParams(collective_id=0, has_side_effects=True, vmem_limit_bytes=20 * 2**20),
         name="reduce_scatter",
     )(acc.reshape(RING, RING, RING, 2, OWNER_ROWS, LANES))
 
 
 def body(a_blocks, p_blocks, a_slot, serve_rows, row_count, contrib_slot, recv_tile):
-    me = lax.axis_index("elem")
-    every = jnp.arange(N, dtype=jnp.int32)
     raw = p_blocks.reshape(R, KP, TILE_ROWS, LANES).transpose(0, 2, 1, 3).reshape(R, B, LANES)
-    rows, outgoing = pl.pallas_call(
-        serve_kernel,
-        grid_spec=pltpu.PrefetchScalarGridSpec(
-            num_scalar_prefetch=1,
-            in_specs=[pl.BlockSpec(memory_space=pltpu.VMEM)],
-            out_specs=(pl.BlockSpec(memory_space=pltpu.VMEM), pl.BlockSpec(memory_space=pltpu.HBM)),
-            scratch_shapes=[pltpu.SemaphoreType.DMA],
-        ),
+    a_native = a_blocks.transpose(1, 0, 2).reshape(KA, R // 8, 8, TILE_ROWS, LANES).transpose(0, 1, 3, 2, 4)
+    tiles = jnp.pad(recv_tile[0], ((0, 0), (0, LANES - CAP))).reshape(N, 1, LANES)
+    block = (RING, RING, RING, 2, S * B, LANES)
+    vmem = pl.BlockSpec(memory_space=pltpu.VMEM)
+    smem = pl.BlockSpec(memory_space=pltpu.SMEM)
+    rows, far, left, told = pl.pallas_call(
+        exchange_kernel,
+        in_specs=[smem, smem, vmem, vmem, pl.BlockSpec(memory_space=pl.ANY)],
+        out_specs=(vmem,) * 4,
         out_shape=(
             pltpu.VMEM((R, B, LANES), jnp.float32),
-            pltpu.HBM((N * S, B, LANES), jnp.float32),
+            pltpu.VMEM(block, jnp.float32),
+            pltpu.VMEM((R, KA, KP * B, LANES), jnp.bfloat16),
+            pltpu.VMEM((N, 1, LANES), jnp.int32),
         ),
-        compiler_params=pltpu.CompilerParams(vmem_limit_bytes=8 * 2**20),
-        name="serve",
-    )(serve_rows[0].T, raw)
-    arrived = lax.all_to_all(outgoing, "elem", split_axis=0, concat_axis=0, tiled=True)
-
-    left = pl.pallas_call(
-        left_kernel,
-        grid_spec=pltpu.PrefetchScalarGridSpec(
-            num_scalar_prefetch=1,
-            grid=(R,),
-            in_specs=[
-                pl.BlockSpec(memory_space=pltpu.VMEM),
-                pl.BlockSpec((1, KA, B, B), lambda i, c: (i, 0, 0, 0)),
-            ],
-            out_specs=pl.BlockSpec((1, KA, KP * B, LANES), lambda i, c: (i, 0, 0, 0), memory_space=pltpu.VMEM),
-        ),
-        out_shape=pltpu.HBM((R, KA, KP * B, LANES), jnp.bfloat16),
-        compiler_params=pltpu.CompilerParams(vmem_limit_bytes=48 * 2**20),
-        cost_estimate=pl.CostEstimate(flops=4 * 2 * R * KA * 128 * 64 * 64, bytes_accessed=16 * 2**20, transcendentals=0),
-        name="left_products",
-    )(row_count, rows, a_blocks.reshape(R, KA, B, B))
-
-    mine = jnp.pad(recv_tile[0], ((0, 0), (0, LANES - CAP))).reshape(N, 1, LANES)
-    told = pl.pallas_call(
-        table_kernel,
-        out_shape=jax.ShapeDtypeStruct((N, 1, LANES), jnp.int32),
-        in_specs=[pl.BlockSpec(memory_space=pltpu.VMEM), pl.BlockSpec(memory_space=pltpu.HBM)],
-        out_specs=pl.BlockSpec(memory_space=pltpu.VMEM),
-        scratch_shapes=[pltpu.SemaphoreType.DMA] * 3,
-        compiler_params=pltpu.CompilerParams(collective_id=1, has_side_effects=True, vmem_limit_bytes=58 * 2**20),
-        cost_estimate=pl.CostEstimate(flops=0, bytes_accessed=2**20, transcendentals=0),
-        name="table",
-    )(mine, left)
-    owner = lax.rem(me + every, N)
-    table = (told[:, 0, :CAP] + owner[:, None] * TO).reshape(N * CAP)
-
-    slot = a_slot.reshape(R * KA)
-    source = lax.rem(me + (2 * N - 1) - (slot - R) // S, N)
-    ext_index = jnp.where(slot < R, slot, R + source * S + (slot - R) % S)
+        scratch_shapes=[
+            pltpu.VMEM(block, jnp.float32),
+            pltpu.VMEM(block, jnp.float32),
+            pltpu.VMEM(block, jnp.float32),
+            pltpu.VMEM((KA * R // 8, 8 * TILE_ROWS, LANES), jnp.float32),
+            *relay_shapes(),
+            pltpu.SemaphoreType.DMA((27 * len(LINES),)),
+            pltpu.SemaphoreType.DMA((27 * len(LINES),)),
+            pltpu.SemaphoreType.DMA((3 * len(LINES),)),
+            *[pltpu.SemaphoreType.DMA] * 4,
+        ],
+        compiler_params=pltpu.CompilerParams(collective_id=1, has_side_effects=True, vmem_limit_bytes=37 * 2**20),
+        name="exchange",
+    )(serve_rows[0].T, row_count, raw, tiles, a_native.reshape(KA * R // 8, 8 * TILE_ROWS, LANES))
     acc = pl.pallas_call(
         tile_kernel,
         grid_spec=pltpu.PrefetchScalarGridSpec(
             num_scalar_prefetch=3,
-            in_specs=[
-                pl.BlockSpec(memory_space=pltpu.HBM),
-                pl.BlockSpec(memory_space=pltpu.VMEM),
-                pl.BlockSpec(memory_space=pltpu.HBM),
-            ],
-            out_specs=pl.BlockSpec(memory_space=pltpu.VMEM),
-            scratch_shapes=[
-                pltpu.VMEM((EXT, B, LANES), jnp.float32),
-                pltpu.VMEM((R, KA, KP * B, LANES), jnp.bfloat16),
-                pltpu.SemaphoreType.DMA((2,)),
-                pltpu.SemaphoreType.DMA((PARTS,)),
-            ],
+            in_specs=[vmem] * 4,
+            out_specs=vmem,
+            scratch_shapes=[pltpu.SMEM((N, 1, LANES), jnp.int32), pltpu.SemaphoreType.DMA],
         ),
         out_shape=pltpu.VMEM((N * TO, TILE_ROWS, LANES), jnp.float32),
-        compiler_params=pltpu.CompilerParams(vmem_limit_bytes=42 * 2**20),
-        cost_estimate=pl.CostEstimate(flops=4 * 2 * R * KA * 128 * 64 * 128, bytes_accessed=34 * 2**20, transcendentals=0),
+        compiler_params=pltpu.CompilerParams(vmem_limit_bytes=2 * 2**20),
         name="tiles",
-    )(ext_index, contrib_slot.reshape(-1), table, left, rows, arrived)
-
-    tiles = reduce_scatter(acc)
-    return tiles.reshape(TO, TILE_ROWS, 2, B).transpose(0, 2, 1, 3).reshape(TO, B * B)
+    )(row_count, a_slot.T, contrib_slot, left, rows, far.reshape(N * S, B, LANES), told)
+
+    summed = reduce_scatter(acc)
+    return summed.reshape(TO, TILE_ROWS, 2, B).transpose(0, 2, 1, 3).reshape(TO, B * B)
 
 
 def solution(mesh):
@@ -432,5 +531,4 @@
         P("elem", None),
         P("elem", None, None),
     )
-
     return jax.shard_map(body, mesh=mesh, in_specs=in_specs, out_specs=P("elem", None), check_vma=False)

time: 198 us -> 186 us (0.939)
  Pallas kernels: 161 us -> 180 us
  local copies, waits for them, and re-layouts: 20.4 us -> 3.85 us
  starting transfers between devices: 12.1 us -> 0 us
    pallas_call x3 -> x1, Pallas kernels: 94 us -> 117 us  [body(): pl.pallas_call(exchange_kernel, in_specs=[smem, smem, vmem, vmem, pl.Bloc...]
    reshape x6 -> x2, local copies, waits for them, and re-layouts: 16.3 us -> 0.96 us  [body(): summed.reshape(TO, TILE_ROWS, 2, B).transpose(0, 2, 1, 3).reshape(TO, B * B)]
    all_to_all x1 -> x0, starting transfers between devices: 12.1 us -> none  [body(): lax.all_to_all(outgoing, 'elem', split_axis=0, concat_axis=0, tiled=True)]
    pallas_call x1, Pallas kernels: 18.6 us -> 11.9 us  [body(): pl.pallas_call(tile_kernel, grid_spec=pltpu.PrefetchScalarGridSpec(num_sc...]
  transfers between devices with their start and end apart: 1 -> 0, of which waited for: 0 -> 0; matrix products, arithmetic and copies ran while one was open for 10% -> 0% of each run, Pallas kernels for 46% -> 0%
where the time goes in v4:
time: 186 us; the launch traced here: 184 us
  Pallas kernels  180 us (97%)
  local copies, waits for them, and re-layouts  3.85 us (2%)
    pallas_call x1, Pallas kernels, body(): pl.pallas_call(exchange_kernel, in_specs=[smem, smem, vmem, vmem, pl.Bloc...  117 us
    pallas_call x1, Pallas kernels, reduce_scatter(): pl.pallas_call(reduce_kernel, out_shape=jax.ShapeDtypeStruct((OWNER_ROWS,...  50.5 us
    pallas_call x1, Pallas kernels, body(): pl.pallas_call(tile_kernel, grid_spec=pltpu.PrefetchScalarGridSpec(num_sc...  11.9 us

profile of v4, /device:TPU:1, one launch (start us, length us, event | category | flops | bytes accessed | tf_op | source)
XLA Modules:
  0.0 184.1 jit_solution(16034826321215129213)
XLA Ops:
  0.7 0.8 copy.9
  1.5 0.0 copy-start.2
  1.5 0.7 copy-done.2
  2.1 117.1 %exchange.1 = (f32[32,64,128]{2,1,0:T(8,128)S(1)}, f32[4,4,4,2,128,128]{5,4,3,2,1,0:T(8,128)S(1)}, bf16[32,7,128,128]{3,2,1,0:T(8,128)(2,1)S(1)}, s32[128,1,128]{2,1,0:T(1,128)S(1)}) custom-call(s32[2,127]{1,0:T(2,128)S(1)} %bitcast.27, s32[1]{0:T(128)S(6)} %copy.11.count_ref, f32[32,64,128]{2,1,0:T(8,128)} %bitcast.30, s32[128,1,128]{2,1,0:T(1,128)S(1)} %bitcast.25, ...), custom_call_target="tpu_custom_call" | custom-call | tf_op jit(solution)/shard_map/exchange/pallas_call | solution.py:483
  119.2 0.0 copy-start
  119.2 0.7 copy-done
  119.9 0.0 copy-start.1
  119.9 0.7 copy-done.1
  120.6 11.9 %tiles.1 = f32[1024,32,128]{2,1,0:T(8,128)S(1)} custom-call(s32[1]{0:T(128)S(6)} %copy.11.count_ref, s32[7,32]{1,0:T(8,128)S(1)} %bitcast.26, s32[32,28]{1,0:T(8,128)S(1)} %copy-done, bf16[32,7,128,128]{3,2,1,0:T(8,128)(2,1)S(1)} %get-tuple-element.9.left_ref, f32[32,64,128]{2,1,0:T(8,128)S(1)} %get-tuple-element.10.own_ref, f32[256,64,128]{2,1,0:T(8,128)S(1)} %bitcast.24, ...), custom_call_target="tpu_custom_call" | custom-call | tf_op jit(solution)/shard_map/tiles/pallas_call | solution.py:507
  132.6 50.5 %reduce_scatter.1 = f32[256,128]{1,0:T(8,128)S(1)} custom-call(f32[4,4,4,2,256,128]{5,4,3,2,1,0:T(8,128)S(1)} %bitcast.23), custom_call_target="tpu_custom_call" | custom-call | tf_op jit(solution)/shard_map/reduce_scatter/pallas_call | solution.py:458
  183.1 0.2 reshape.34
  183.3 0.8 reshape.35
  (2 shorter events, 0.0 us)
Async XLA Ops:
  1.5 0.7 copy-start.2
  119.2 0.7 copy-start
  119.9 0.7 copy-start.1

commit v5 on v4

--- a/solution.py
+++ b/solution.py
@@ -23,6 +23,7 @@
 GROUPS = ((0, 40), (40, 48), (88, 40), (128, 48), (176, 40), (216, 40))
 ORDERS = ((0, 1, 2), (1, 2, 0), (2, 0, 1)) * 2
 SETS = ((0, 1, 2), (3, 4, 5))
+AHEAD = 6
 
 
 def split(value):
@@ -31,7 +32,9 @@
     return high, low
 
 
-LINES = ((0, 24), (24, 24), (48, 16), (64, 16), (80, 24), (104, 24))
+LINES = ((0, 16), (16, 16), (32, 16), (48, 16), (64, 8), (72, 16), (88, 8), (96, 16), (112, 16))
+LINE_ORDERS = ((0, 1, 2), (1, 2, 0), (2, 0, 1)) * 3
+LINE_SETS = ((0, 1, 2), (3, 4, 5), (6, 7, 8))
 SHARES = (8, 8, 6, 6, 4)
 
 
@@ -39,10 +42,10 @@
     return [pltpu.VMEM((RING, RING, length, LANES), jnp.float32) for _, length in LINES for _ in range(6)]
 
 
-def exchange_kernel(serve_ref, count_ref, raw_ref, tiles_ref, a_hbm, rows_ref, far_ref, left_ref, told_ref, *rest):
-    out, first_hop, second_hop, a_ref = rest[:4]
-    relays = rest[4:40]
-    send, recv, local, a_sem, told_send, told_recv, told_own = rest[40:]
+def exchange_kernel(serve_ref, count_ref, raw_ref, tiles_ref, a_hbm, slot_hbm, row_hbm, rows_ref, far_ref, left_ref, told_ref, slot_ref, row_ref, *rest):
+    out, first_hop, second_hop, a_ref, turned_ref, first_told, second_told, third_told = rest[:8]
+    relays = rest[8:-7]
+    send, recv, local, pass_sem, told_send, told_recv, told_local = rest[-7:]
     hops = (out, first_hop, second_hop, far_ref)
     me = lax.axis_index("elem")
     core = me % 2
@@ -56,15 +59,16 @@
 
     barrier = pltpu.get_barrier_semaphore()
 
-    def greet(m, carry):
-        pl.semaphore_signal(barrier, inc=1, device_id=(lax.rem(me + m, N),), device_id_type=MESH)
-        return carry
-
-    lax.fori_loop(1, N, greet, 0)
-    a_copy = pltpu.make_async_copy(a_hbm, a_ref, a_sem)
-    a_copy.start()
-    own_tiles = pltpu.make_async_copy(tiles_ref.at[0], told_ref.at[0], told_own)
-    own_tiles.start()
+    near = [device_at(0, 0, 1 - core)]
+    near += [device_at(axis, step, k) for axis in range(3) for step in (1, 2, 3) for k in range(2)]
+    for other in near:
+        pl.semaphore_signal(barrier, inc=1, device_id=(other,), device_id_type=MESH)
+    passing = [
+        pltpu.make_async_copy(source, target, pass_sem.at[n])
+        for n, (source, target) in enumerate(((a_hbm, a_ref), (slot_hbm, slot_ref), (row_hbm, row_ref)))
+    ]
+    for copy in passing:
+        copy.start()
 
     lane = lax.broadcasted_iota(jnp.int32, (B, LANES), 1) < B
     even = lax.broadcasted_iota(jnp.int32, (B, LANES), 0) % 2 == 0
@@ -77,33 +81,89 @@
         return carry
 
     lax.fori_loop(0, R, turn, 0)
-
-    def place_of(device):
-        return device // (2 * RING * RING), (device // (2 * RING)) % RING, (device // 2) % RING, device % 2
+    turned_ref[...] = jnp.zeros((N, LANES), jnp.int32)
+    turned_ref[0:CAP, :] = tiles_ref[...]
+    turned_ref[...] = turned_ref[...].T
 
     def gather(n, carry):
-        y, x, z, k = place_of(lax.rem(me + 1 + n, N))
-        for c in range(S):
-            out[y, x, z, k, c * B : (c + 1) * B, :] = rows_ref[serve_ref[c, n]]
+        y, x = n // RING, n % RING
+        for z in range(RING):
+            for k in range(2):
+                ahead = lax.rem(n * (2 * RING) + (2 * z + k) + N - me, N)
+                for c in range(S):
+                    out[y, x, z, k, c * B : (c + 1) * B, :] = rows_ref[serve_ref[c, lax.rem(ahead + N - 2, N - 1)]]
+                first_told[y, x, z, k] = turned_ref[pl.ds(lax.rem(N - ahead, N), 1), :]
         return carry
 
-    lax.fori_loop(0, N - 1, gather, 0)
-    out[place[0], place[1], place[2], core] = jnp.zeros((S * B, LANES), jnp.float32)
-    pl.semaphore_wait(barrier, N - 1)
-
-    def tell(m, carry):
-        pltpu.make_async_remote_copy(
-            src_ref=tiles_ref.at[m],
-            dst_ref=told_ref.at[m],
-            send_sem=told_send,
-            recv_sem=told_recv,
-            device_id=(lax.rem(me + N - m, N),),
-            device_id_type=MESH,
-        ).start()
-        return carry
-
-    lax.fori_loop(1, N, tell, 0)
-
+    lax.fori_loop(0, RING * RING, gather, 0)
+    pl.semaphore_wait(barrier, len(near))
+    tolds = (first_told, second_told, third_told, told_ref)
+
+    def tell(phase):
+        source, target = tolds[phase], tolds[phase + 1]
+        u = place[phase]
+
+        def at(index, core_at=slice(None)):
+            spot = [slice(None)] * 3
+            spot[phase] = index
+            return tuple(spot) + (core_at, slice(None), slice(None))
+
+        flights = []
+        for step in range(RING):
+            for part in range(2 if phase == 2 else 1):
+                to = (u + step) % RING
+                if phase == 2:
+                    src, dst = source.at[at(to, part)], target.at[at(u, core)]
+                    device = device_at(phase, step, part)
+                else:
+                    src, dst = source.at[at(to)], target.at[at(u)]
+                    device = device_at(phase, step, core)
+                if phase == 2 and step == 0:
+                    continue
+                if step == 0:
+                    copy = pltpu.make_async_copy(src, dst, told_local.at[phase])
+                    copy.start()
+                    told_waits.append((phase, copy.wait))
+                    continue
+                lane_of = phase * 8 + 2 * step + (core if phase == 2 else 0)
+                copy = pltpu.make_async_remote_copy(
+                    src_ref=src,
+                    dst_ref=dst,
+                    send_sem=told_send.at[phase * 8 + 2 * step + part],
+                    recv_sem=told_recv.at[lane_of],
+                    device_id=(device,),
+                    device_id_type=MESH,
+                )
+                copy.start()
+                sent.append(copy)
+        if phase == 2:
+            copy = pltpu.make_async_copy(source.at[at(u, core)], target.at[at(u, core)], told_local.at[2])
+            copy.start()
+            told_waits.append((phase, copy.wait))
+            copy = pltpu.make_async_remote_copy(
+                src_ref=source.at[at(u, 1 - core)],
+                dst_ref=target.at[at(u, core)],
+                send_sem=told_send.at[phase * 8],
+                recv_sem=told_recv.at[phase * 8],
+                device_id=(device_at(phase, 0, 1 - core),),
+                device_id_type=MESH,
+            )
+            copy.start()
+            sent.append(copy)
+
+    def told_wait(phase):
+        target = tolds[phase + 1]
+        for at_phase, wait in told_waits:
+            if at_phase == phase:
+                wait()
+        spot = [slice(None)] * 3
+        spot[phase] = place[phase]
+        lanes = (0, 2, 3, 4, 5, 6, 7) if phase == 2 else (2, 4, 6)
+        like = target.at[tuple(spot) + ((core if phase == 2 else slice(None)), slice(None), slice(None))]
+        for lane_of in lanes:
+            pltpu.make_async_copy(like, like, told_recv.at[phase * 8 + lane_of]).wait()
+
+    told_waits = []
     def window(group, axis, at_axis, core_at):
         at = [slice(None)] * 3
         at[axis] = at_axis
@@ -131,7 +191,7 @@
     def first_wave(groups, phase):
         source, target = hops[phase], hops[phase + 1]
         for group in groups:
-            axis = ORDERS[group][phase]
+            axis = LINE_ORDERS[group][phase]
             u = place[axis]
             for part, step in ((0, 1), (1, 3)):
                 relay = relays[(group * 3 + phase) * 2 + part]
@@ -139,7 +199,7 @@
                 fly(group, phase, part, src, relay, device_at(axis, step, core), part)
         for side, step in ((0, 1), (1, 3)):
             for group in groups:
-                axis = ORDERS[group][phase]
+                axis = LINE_ORDERS[group][phase]
                 u = place[axis]
                 to = (u + step) % RING
                 if phase < 2:
@@ -152,7 +212,7 @@
                         src = source.at[window(group, axis, to, part)]
                         fly(group, phase, kind, src, target.at[at], device_at(axis, step, part), 2 + 2 * side + core)
         for group in groups:
-            axis = ORDERS[group][phase]
+            axis = LINE_ORDERS[group][phase]
             u = place[axis]
             at = window(group, axis, u, None if phase < 2 else core)
             keep = pltpu.make_async_copy(source.at[at], target.at[at], local.at[group * 3 + phase])
@@ -165,7 +225,7 @@
     def second_wave(groups, phase):
         target = hops[phase + 1]
         for group in groups:
-            axis = ORDERS[group][phase]
+            axis = LINE_ORDERS[group][phase]
             u = place[axis]
             for part, step in ((0, 1), (1, 3)):
                 relay = relays[(group * 3 + phase) * 2 + part]
@@ -181,7 +241,7 @@
     def third_wave(groups, phase):
         target = hops[phase + 1]
         for group in groups:
-            axis = ORDERS[group][phase]
+            axis = LINE_ORDERS[group][phase]
             u = place[axis]
             arrivals[group, phase].wait()
             for side in range(2):
@@ -217,40 +277,45 @@
         done = sum(SHARES[:n])
         lax.fori_loop(done, done + SHARES[n], left_row, 0)
 
-    for groups in SETS:
+    for groups in LINE_SETS:
         first_wave(groups, 0)
-    a_copy.wait()
+    tell(0)
+    for copy in passing:
+        copy.wait()
     left_share(0)
     for phase in range(3):
-        for groups in SETS:
+        for groups in LINE_SETS:
             second_wave(groups, phase)
         if phase < 2:
             left_share(2 * phase + 1)
-        for groups in SETS:
+        for groups in LINE_SETS:
             third_wave(groups, phase)
             if phase < 2:
                 first_wave(groups, phase + 1)
+        told_wait(phase)
         if phase < 2:
+            tell(phase + 1)
             left_share(2 * phase + 2)
-    own_tiles.wait()
-    others = pl.ds(1, N - 1)
-    pltpu.make_async_copy(tiles_ref.at[others], tiles_ref.at[others], told_send).wait()
-    pltpu.make_async_copy(told_ref.at[others], told_ref.at[others], told_recv).wait()
     for copy in sent:
         copy.wait_send()
 
 
-def tile_kernel(count_ref, row_ref, slot_ref, left_ref, own_ref, far_ref, told_ref, acc, told, told_sem):
+def tile_kernel(count_ref, left_ref, own_ref, far_ref, told_in, slot_in, row_in, acc, told, slot_ref, row_ref, sem):
     me = lax.axis_index("elem")
-    told_copy = pltpu.make_async_copy(told_ref, told, told_sem)
-    told_copy.start()
+    tables = [
+        pltpu.make_async_copy(source, target, sem.at[n])
+        for n, (source, target) in enumerate(((told_in, told), (slot_in, slot_ref), (row_in, row_ref)))
+    ]
+    for copy in tables:
+        copy.start()
 
     def clear(n, carry):
         acc[pl.ds(n * 8, 8)] = jnp.zeros((8, TILE_ROWS, LANES), jnp.float32)
         return carry
 
     lax.fori_loop(0, N * TO // 8, clear, 0)
-    told_copy.wait()
+    for copy in tables:
+        copy.wait()
     lane = lax.broadcasted_iota(jnp.int32, (TILE_ROWS, LANES), 1)
 
     def step(row, carry):
@@ -258,7 +323,7 @@
             index = row_ref[k, row]
             away = jnp.maximum(index - R, 0)
             own = own_ref[jnp.minimum(index, R - 1)]
-            far = far_ref[((me + 2 * N - 1 - away // S) % N) * S + away % S]
+            far = far_ref[lax.rem(me + 2 * N - 1 - lax.div(away, S), N) * S + lax.rem(away, S)]
             high, low = split(jnp.where(index < R, own, far))
             wide = jnp.concatenate([high, low], axis=1)
             both = jnp.dot(left_ref[row, k], jnp.concatenate([wide, wide], axis=0), preferred_element_type=jnp.float32)
@@ -271,8 +336,8 @@
                 tiles = (jnp.where(lane < B, upper, lower_t), jnp.where(lane < B, upper_t, lower))
                 for q in range(KP):
                     slot = slot_ref[row, p * (KA * KP) + k * KP + q]
-                    position = slot // CAP
-                    target = ((me + position) % N) * TO + told[position, 0, slot % CAP]
+                    owner = lax.rem(me + lax.div(slot, CAP), N)
+                    target = owner * TO + told[owner, 0, lax.rem(slot, CAP)]
                     acc[target] += tiles[q]
         return carry
 
@@ -290,27 +355,27 @@
 
 
 def add(target, *terms):
-    lead = target.shape[:-2]
-    total = 1
-    for size in lead:
-        total *= size
-
-    def one(n, carry):
-        at = []
-        for size in reversed(lead):
-            at.insert(0, n % size)
-            n = n // size
-        at = tuple(at) + (slice(None), slice(None))
+    def one(at):
         value = target[at]
         for term in terms:
             value = value + term[at]
         target[at] = value
+
+    lead = target.shape[:-2]
+    whole = (slice(None), slice(None))
+    if not lead:
+        one(whole)
+        return
+
+    def outer(n, carry):
+        if len(lead) == 1:
+            one((n,) + whole)
+        else:
+            for m in range(lead[1]):
+                one((n, m) + whole)
         return carry
 
-    if total == 1:
-        one(0, 0)
-    else:
-        lax.fori_loop(0, total, one, 0)
+    lax.fori_loop(0, lead[0], outer, 0)
 
 
 def reduce_kernel(acc_ref, out_ref, mine, *rest):
@@ -353,30 +418,39 @@
         at, _ = window(group, fixed, None)
         return at[:3] + (core_at,) + at[3:]
 
-    loads = {}
-    for groups, offset in ((0, 2), (0, 1), (0, 3), (1, 2), (1, 1), (1, 3), (0, 0), (1, 0)):
-        for group in SETS[groups]:
-            axis = ORDERS[group][0]
-            fixed = {axis: (place[axis] + offset) % RING}
-            n = group * RING + offset
-            at, _ = window(group, fixed, None)
-            give = pltpu.make_async_remote_copy(
-                src_ref=acc_ref.at[across(group, fixed, 1 - core)],
-                dst_ref=mine.at[at],
-                send_sem=in_send.at[n],
-                recv_sem=in_recv.at[n],
-                device_id=(partner,),
-                device_id_type=MESH,
-            )
-            give.start()
-            loads[group, offset] = (give, acc_ref.at[across(group, fixed, core)], mine.at[at])
+    queue = [(n, step) for n in range(len(SETS)) for step in (2, 1, 3)] + [(n, 0) for n in range(len(SETS))]
+    queue = [(group, step) for n, step in queue for group in SETS[n]]
+    loads, sends = {}, []
+
+    def fetch():
+        if len(loads) == len(queue):
+            return
+        group, offset = queue[len(loads)]
+        axis = ORDERS[group][0]
+        fixed = {axis: (place[axis] + offset) % RING}
+        n = group * RING + offset
+        at, _ = window(group, fixed, None)
+        give = pltpu.make_async_remote_copy(
+            src_ref=acc_ref.at[across(group, fixed, 1 - core)],
+            dst_ref=mine.at[at],
+            send_sem=in_send.at[n],
+            recv_sem=in_recv.at[n],
+            device_id=(partner,),
+            device_id_type=MESH,
+        )
+        give.start()
+        loads[group, offset] = (give, acc_ref.at[across(group, fixed, core)], mine.at[at])
+        sends.append(give)
+
+    for _ in range(AHEAD):
+        fetch()
 
     def arrive(group, offset):
         give, own, target = loads[group, offset]
         give.wait_recv()
+        fetch()
         add(target, own)
 
-    sends = [give for give, _, _ in loads.values()]
     flights = {}
 
     def fixed_at(group, stage, step):
@@ -476,46 +550,58 @@
 def body(a_blocks, p_blocks, a_slot, serve_rows, row_count, contrib_slot, recv_tile):
     raw = p_blocks.reshape(R, KP, TILE_ROWS, LANES).transpose(0, 2, 1, 3).reshape(R, B, LANES)
     a_native = a_blocks.transpose(1, 0, 2).reshape(KA, R // 8, 8, TILE_ROWS, LANES).transpose(0, 1, 3, 2, 4)
-    tiles = jnp.pad(recv_tile[0], ((0, 0), (0, LANES - CAP))).reshape(N, 1, LANES)
     block = (RING, RING, RING, 2, S * B, LANES)
+    told_block = (RING, RING, RING, 2, 1, LANES)
     vmem = pl.BlockSpec(memory_space=pltpu.VMEM)
     smem = pl.BlockSpec(memory_space=pltpu.SMEM)
-    rows, far, left, told = pl.pallas_call(
+    rows, far, left, told, slots, slot_rows = pl.pallas_call(
         exchange_kernel,
-        in_specs=[smem, smem, vmem, vmem, pl.BlockSpec(memory_space=pl.ANY)],
-        out_specs=(vmem,) * 4,
+        in_specs=[smem, smem, vmem, vmem] + [pl.BlockSpec(memory_space=pl.ANY)] * 3,
+        out_specs=(vmem,) * 6,
         out_shape=(
             pltpu.VMEM((R, B, LANES), jnp.float32),
             pltpu.VMEM(block, jnp.float32),
             pltpu.VMEM((R, KA, KP * B, LANES), jnp.bfloat16),
-            pltpu.VMEM((N, 1, LANES), jnp.int32),
+            pltpu.VMEM(told_block, jnp.int32),
+            pltpu.VMEM((R, KP * KA * KP), jnp.int32),
+            pltpu.VMEM((KA, R), jnp.int32),
         ),
         scratch_shapes=[
             pltpu.VMEM(block, jnp.float32),
             pltpu.VMEM(block, jnp.float32),
             pltpu.VMEM(block, jnp.float32),
             pltpu.VMEM((KA * R // 8, 8 * TILE_ROWS, LANES), jnp.float32),
+            pltpu.VMEM((N, LANES), jnp.int32),
+            *[pltpu.VMEM(told_block, jnp.int32)] * 3,
             *relay_shapes(),
             pltpu.SemaphoreType.DMA((27 * len(LINES),)),
             pltpu.SemaphoreType.DMA((27 * len(LINES),)),
             pltpu.SemaphoreType.DMA((3 * len(LINES),)),
-            *[pltpu.SemaphoreType.DMA] * 4,
+            pltpu.SemaphoreType.DMA((3,)),
+            pltpu.SemaphoreType.DMA((24,)),
+            pltpu.SemaphoreType.DMA((24,)),
+            pltpu.SemaphoreType.DMA((3,)),
         ],
-        compiler_params=pltpu.CompilerParams(collective_id=1, has_side_effects=True, vmem_limit_bytes=37 * 2**20),
+        compiler_params=pltpu.CompilerParams(collective_id=1, has_side_effects=True, vmem_limit_bytes=50100000),
         name="exchange",
-    )(serve_rows[0].T, row_count, raw, tiles, a_native.reshape(KA * R // 8, 8 * TILE_ROWS, LANES))
+    )(serve_rows[0].T, row_count, raw, recv_tile[0].T, a_native.reshape(KA * R // 8, 8 * TILE_ROWS, LANES), contrib_slot, a_slot.T)
     acc = pl.pallas_call(
         tile_kernel,
         grid_spec=pltpu.PrefetchScalarGridSpec(
-            num_scalar_prefetch=3,
-            in_specs=[vmem] * 4,
+            num_scalar_prefetch=1,
+            in_specs=[vmem] * 6,
             out_specs=vmem,
-            scratch_shapes=[pltpu.SMEM((N, 1, LANES), jnp.int32), pltpu.SemaphoreType.DMA],
+            scratch_shapes=[
+                pltpu.SMEM((N, 1, LANES), jnp.int32),
+                pltpu.SMEM((R, KP * KA * KP), jnp.int32),
+                pltpu.SMEM((KA, R), jnp.int32),
+                pltpu.SemaphoreType.DMA((3,)),
+            ],
         ),
         out_shape=pltpu.VMEM((N * TO, TILE_ROWS, LANES), jnp.float32),
         compiler_params=pltpu.CompilerParams(vmem_limit_bytes=2 * 2**20),
         name="tiles",
-    )(row_count, a_slot.T, contrib_slot, left, rows, far.reshape(N * S, B, LANES), told)
+    )(row_count, left, rows, far.reshape(N * S, B, LANES), told.reshape(N, 1, LANES), slots, slot_rows)
 
     summed = reduce_scatter(acc)
     return summed.reshape(TO, TILE_ROWS, 2, B).transpose(0, 2, 1, 3).reshape(TO, B * B)

time: 186 us -> 175 us (0.941)
  Pallas kernels: 180 us -> 173 us
  local copies, waits for them, and re-layouts: 3.85 us -> 0.98 us
    pallas_call x1, Pallas kernels: 117 us -> 110 us  [body(): pl.pallas_call(exchange_kernel, in_specs=[smem, smem, vmem, vmem] + [pl.B...]
    pallas_call x1, Pallas kernels: 50.5 us -> 57.1 us  [reduce_scatter(): pl.pallas_call(reduce_kernel, out_shape=jax.ShapeDtypeStruct((OWNER_ROWS,...]
    pallas_call x1, Pallas kernels: 11.9 us -> 6.02 us  [body(): pl.pallas_call(tile_kernel, grid_spec=pltpu.PrefetchScalarGridSpec(num_sc...]
    unnamed x7 -> x0, local copies, waits for them, and re-layouts: 2.86 us -> none
where the time goes in v5:
time: 175 us
  Pallas kernels  173 us (99%)
    pallas_call x1, Pallas kernels, body(): pl.pallas_call(exchange_kernel, in_specs=[smem, smem, vmem, vmem] + [pl.B...  110 us
    pallas_call x1, Pallas kernels, reduce_scatter(): pl.pallas_call(reduce_kernel, out_shape=jax.ShapeDtypeStruct((OWNER_ROWS,...  57.1 us
    pallas_call x1, Pallas kernels, body(): pl.pallas_call(tile_kernel, grid_spec=pltpu.PrefetchScalarGridSpec(num_sc...  6.02 us

profile of v5, /device:TPU:1, one launch (start us, length us, event | category | flops | bytes accessed | tf_op | source)
XLA Modules:
  0.0 174.8 jit_solution(5339654106826714346)
XLA Ops:
  0.7 110.0 %exchange.1 = (f32[32,64,128]{2,1,0:T(8,128)S(1)}, f32[4,4,4,2,128,128]{5,4,3,2,1,0:T(8,128)S(1)}, bf16[32,7,128,128]{3,2,1,0:T(8,128)(2,1)S(1)}, s32[4,4,4,2,1,...) custom-call(s32[2,127]{1,0:T(2,128)} %bitcast.33, s32[1]{0:T(128)S(6)} %copy.10.count_ref, ...), custom_call_target="tpu_custom_call" | custom-call | tf_op jit(solution)/shard_map/exchange/pallas_call | solution.py:557
  110.6 6.0 %tiles.1 = f32[1024,32,128]{2,1,0:T(8,128)S(1)} custom-call(s32[1]{0:T(128)S(6)} %copy.10.count_ref, bf16[32,7,128,128]{3,2,1,0:T(8,128)(2,1)S(1)} %get-tuple-element.11.left_ref, f32[32,64,128]{2,1,0:T(8,128)S(1)} %get-tuple-element.12.own_ref, f32[256,64,128]{2,1,0:T(8,128)S(1)} %bitcast.26, s32[128,1,128]{2,1,0:T(1,128)S(1)} %bitcast.27, ...), custom_call_target="tpu_custom_call" | custom-call | tf_op jit(solution)/shard_map/tiles/pallas_call | solution.py:588
  116.7 57.1 %reduce_scatter.1 = f32[256,128]{1,0:T(8,128)S(1)} custom-call(f32[4,4,4,2,256,128]{5,4,3,2,1,0:T(8,128)S(1)} %bitcast.25), custom_call_target="tpu_custom_call" | custom-call | tf_op jit(solution)/shard_map/reduce_scatter/pallas_call | solution.py:532
  173.8 0.2 reshape.34
  174.0 0.8 reshape.35
  (1 shorter events, 0.0 us)

commit v6 on v5

--- a/solution.py
+++ b/solution.py
@@ -288,6 +288,9 @@
             second_wave(groups, phase)
         if phase < 2:
             left_share(2 * phase + 1)
+        if phase == 2:
+            for copy in sent:
+                copy.wait_send()
         for groups in LINE_SETS:
             third_wave(groups, phase)
             if phase < 2:
@@ -296,8 +299,6 @@
         if phase < 2:
             tell(phase + 1)
             left_share(2 * phase + 2)
-    for copy in sent:
-        copy.wait_send()
 
 
 def tile_kernel(count_ref, left_ref, own_ref, far_ref, told_in, slot_in, row_in, acc, told, slot_ref, row_ref, sem):
@@ -341,7 +342,14 @@
                     acc[target] += tiles[q]
         return carry
 
-    lax.fori_loop(0, jnp.minimum(count_ref[0], R), step, 0)
+    count = jnp.minimum(count_ref[0], R)
+
+    def pair(n, carry):
+        step(2 * n, carry)
+        return step(2 * n + 1, carry)
+
+    lax.fori_loop(0, lax.div(count, 2), pair, 0)
+    lax.fori_loop(lax.div(count, 2) * 2, count, step, 0)
 
 
 def ring_shapes():
@@ -482,10 +490,12 @@
                 for kind, part, towards, buffer in sends_of:
                     start(group, stage, kind, step, part, towards, buffer)
 
-    def last_wave(groups):
+    def last_sends(groups):
         for kind, step in ((1, 2), (0, 1), (2, 3)):
             for group in groups:
                 start(group, 2, kind, step, None, step, kind)
+
+    def finish(groups):
         for group in groups:
             for kind in range(3):
                 flights[group, 2, kind].wait_recv()
@@ -522,10 +532,12 @@
                 third_wave(group, stage)
             if stage == 0:
                 first_wave(groups, 1)
-    for groups in SETS:
-        last_wave(groups)
+            else:
+                last_sends(groups)
     for copy in sends:
         copy.wait_send()
+    for groups in SETS:
+        finish(groups)
 
 
 def reduce_scatter(acc):

time: 175 us -> 170 us (0.971)
  Pallas kernels: 173 us -> 166 us
    pallas_call x1, Pallas kernels: 57.1 us -> 49.5 us  [reduce_scatter(): pl.pallas_call(reduce_kernel, out_shape=jax.ShapeDtypeStruct((OWNER_ROWS,...]
where the time goes in v6:
time: 170 us; the launch traced here: 168 us
  Pallas kernels  166 us (98%)
    pallas_call x1, Pallas kernels, body(): pl.pallas_call(exchange_kernel, in_specs=[smem, smem, vmem, vmem] + [pl.B...  110 us
    pallas_call x1, Pallas kernels, reduce_scatter(): pl.pallas_call(reduce_kernel, out_shape=jax.ShapeDtypeStruct((OWNER_ROWS,...  49.5 us
    pallas_call x1, Pallas kernels, body(): pl.pallas_call(tile_kernel, grid_spec=pltpu.PrefetchScalarGridSpec(num_sc...  7.28 us

profile of v6, /device:TPU:1, one launch (start us, length us, event | category | flops | bytes accessed | tf_op | source)
XLA Modules:
  0.0 168.1 jit_solution(15016122877761401070)
XLA Ops:
  0.7 109.7 %exchange.1 = (f32[32,64,128]{2,1,0:T(8,128)S(1)}, f32[4,4,4,2,128,128]{5,4,3,2,1,0:T(8,128)S(1)}, bf16[32,7,128,128]{3,2,1,0:T(8,128)(2,1)S(1)}, s32[4,4,4,2,1,...) custom-call(s32[2,127]{1,0:T(2,128)} %bitcast.33, s32[1]{0:T(128)S(6)} %copy.10.count_ref, ...), custom_call_target="tpu_custom_call" | custom-call | tf_op jit(solution)/shard_map/exchange/pallas_call | solution.py:569
  110.3 7.3 %tiles.1 = f32[1024,32,128]{2,1,0:T(8,128)S(1)} custom-call(s32[1]{0:T(128)S(6)} %copy.10.count_ref, bf16[32,7,128,128]{3,2,1,0:T(8,128)(2,1)S(1)} %get-tuple-element.11.left_ref, f32[32,64,128]{2,1,0:T(8,128)S(1)} %get-tuple-element.12.own_ref, f32[256,64,128]{2,1,0:T(8,128)S(1)} %bitcast.26, s32[128,1,128]{2,1,0:T(1,128)S(1)} %bitcast.27, ...), custom_call_target="tpu_custom_call" | custom-call | tf_op jit(solution)/shard_map/tiles/pallas_call | solution.py:600
  117.6 49.5 %reduce_scatter.1 = f32[256,128]{1,0:T(8,128)S(1)} custom-call(f32[4,4,4,2,256,128]{5,4,3,2,1,0:T(8,128)S(1)} %bitcast.25), custom_call_target="tpu_custom_call" | custom-call | tf_op jit(solution)/shard_map/reduce_scatter/pallas_call | solution.py:544
  167.1 0.2 reshape.34
  167.3 0.8 reshape.35
  (1 shorter events, 0.0 us)

commit v7 on v6

--- a/solution.py
+++ b/solution.py
@@ -344,12 +344,13 @@
 
     count = jnp.minimum(count_ref[0], R)
 
-    def pair(n, carry):
-        step(2 * n, carry)
-        return step(2 * n + 1, carry)
-
-    lax.fori_loop(0, lax.div(count, 2), pair, 0)
-    lax.fori_loop(lax.div(count, 2) * 2, count, step, 0)
+    def eight(n, carry):
+        for m in range(8):
+            step(8 * n + m, carry)
+        return carry
+
+    lax.fori_loop(0, lax.div(count, 8), eight, 0)
+    lax.fori_loop(lax.div(count, 8) * 8, count, step, 0)
 
 
 def ring_shapes():

time: 170 us -> 168 us (0.988)
  Pallas kernels: 166 us -> 164 us
    pallas_call x1, Pallas kernels: 7.28 us -> 5.31 us  [body(): pl.pallas_call(tile_kernel, grid_spec=pltpu.PrefetchScalarGridSpec(num_sc...]
where the time goes in v7:
time: 168 us; the launch traced here: 166 us
  Pallas kernels  164 us (98%)
    pallas_call x1, Pallas kernels, body(): pl.pallas_call(exchange_kernel, in_specs=[smem, smem, vmem, vmem] + [pl.B...  110 us
    pallas_call x1, Pallas kernels, reduce_scatter(): pl.pallas_call(reduce_kernel, out_shape=jax.ShapeDtypeStruct((OWNER_ROWS,...  49.4 us
    pallas_call x1, Pallas kernels, body(): pl.pallas_call(tile_kernel, grid_spec=pltpu.PrefetchScalarGridSpec(num_sc...  5.31 us

profile of v7, /device:TPU:1, one launch (start us, length us, event | category | flops | bytes accessed | tf_op | source)
XLA Modules:
  0.0 166.0 jit_solution(1776084507448574378)
XLA Ops:
  0.7 109.7 %exchange.1 = (f32[32,64,128]{2,1,0:T(8,128)S(1)}, f32[4,4,4,2,128,128]{5,4,3,2,1,0:T(8,128)S(1)}, bf16[32,7,128,128]{3,2,1,0:T(8,128)(2,1)S(1)}, s32[4,4,4,2,1,...) custom-call(s32[2,127]{1,0:T(2,128)} %bitcast.33, s32[1]{0:T(128)S(6)} %copy.10.count_ref, ...), custom_call_target="tpu_custom_call" | custom-call | tf_op jit(solution)/shard_map/exchange/pallas_call | solution.py:570
  110.3 5.3 %tiles.1 = f32[1024,32,128]{2,1,0:T(8,128)S(1)} custom-call(s32[1]{0:T(128)S(6)} %copy.10.count_ref, bf16[32,7,128,128]{3,2,1,0:T(8,128)(2,1)S(1)} %get-tuple-element.11.left_ref, f32[32,64,128]{2,1,0:T(8,128)S(1)} %get-tuple-element.12.own_ref, f32[256,64,128]{2,1,0:T(8,128)S(1)} %bitcast.26, s32[128,1,128]{2,1,0:T(1,128)S(1)} %bitcast.27, ...), custom_call_target="tpu_custom_call" | custom-call | tf_op jit(solution)/shard_map/tiles/pallas_call | solution.py:601
  115.6 49.4 %reduce_scatter.1 = f32[256,128]{1,0:T(8,128)S(1)} custom-call(f32[4,4,4,2,256,128]{5,4,3,2,1,0:T(8,128)S(1)} %bitcast.25), custom_call_target="tpu_custom_call" | custom-call | tf_op jit(solution)/shard_map/reduce_scatter/pallas_call | solution.py:545
  165.0 0.2 reshape.34
  165.2 0.8 reshape.35
  (1 shorter events, 0.0 us)

commit v8 on v7

--- a/solution.py
+++ b/solution.py
@@ -291,10 +291,10 @@
         if phase == 2:
             for copy in sent:
                 copy.wait_send()
-        for groups in LINE_SETS:
-            third_wave(groups, phase)
+        for group in range(len(LINES)):
+            third_wave((group,), phase)
             if phase < 2:
-                first_wave(groups, phase + 1)
+                first_wave((group,), phase + 1)
         told_wait(phase)
         if phase < 2:
             tell(phase + 1)
@@ -335,11 +335,14 @@
                 upper, lower = part[top : top + TILE_ROWS], part[bottom : bottom + TILE_ROWS]
                 upper_t, lower_t = turned[top : top + TILE_ROWS], turned[bottom : bottom + TILE_ROWS]
                 tiles = (jnp.where(lane < B, upper, lower_t), jnp.where(lane < B, upper_t, lower))
+                targets = []
                 for q in range(KP):
                     slot = slot_ref[row, p * (KA * KP) + k * KP + q]
                     owner = lax.rem(me + lax.div(slot, CAP), N)
-                    target = owner * TO + told[owner, 0, lax.rem(slot, CAP)]
-                    acc[target] += tiles[q]
+                    targets.append(owner * TO + told[owner, 0, lax.rem(slot, CAP)])
+                first, second = (acc[target] for target in targets)
+                acc[targets[0]] = first + tiles[0]
+                acc[targets[1]] = second + (tiles[1] + jnp.where(targets[0] == targets[1], tiles[0], 0.0))
         return carry
 
     count = jnp.minimum(count_ref[0], R)
@@ -526,15 +529,15 @@
         for groups in SETS:
             for group in groups:
                 second_wave(group, stage)
-        for groups in SETS:
-            for group in groups:
-                if stage == 0:
-                    arrive(group, 0)
-                third_wave(group, stage)
+        if stage == 0:
+            for group in range(len(GROUPS)):
+                arrive(group, 0)
+        for group in range(len(GROUPS)):
+            third_wave(group, stage)
             if stage == 0:
-                first_wave(groups, 1)
+                first_wave((group,), 1)
             else:
-                last_sends(groups)
+                last_sends((group,))
     for copy in sends:
         copy.wait_send()
     for groups in SETS:

time: 168 us -> 166 us (0.988); the launches traced: 166 us -> 166 us
    pallas_call x1, Pallas kernels: 5.31 us -> 9.07 us  [body(): pl.pallas_call(tile_kernel, grid_spec=pltpu.PrefetchScalarGridSpec(num_sc...]
    pallas_call x1, Pallas kernels: 49.4 us -> 45.8 us  [reduce_scatter(): pl.pallas_call(reduce_kernel, out_shape=jax.ShapeDtypeStruct((OWNER_ROWS,...]
where the time goes in v8:
time: 166 us
  Pallas kernels  165 us (99%)
    pallas_call x1, Pallas kernels, body(): pl.pallas_call(exchange_kernel, in_specs=[smem, smem, vmem, vmem] + [pl.B...  110 us
    pallas_call x1, Pallas kernels, reduce_scatter(): pl.pallas_call(reduce_kernel, out_shape=jax.ShapeDtypeStruct((OWNER_ROWS,...  45.8 us
    pallas_call x1, Pallas kernels, body(): pl.pallas_call(tile_kernel, grid_spec=pltpu.PrefetchScalarGridSpec(num_sc...  9.07 us

profile of v8, /device:TPU:1, one launch (start us, length us, event | category | flops | bytes accessed | tf_op | source)
XLA Modules:
  0.0 166.2 jit_solution(3288801377171658692)
XLA Ops:
  0.7 109.6 %exchange.1 = (f32[32,64,128]{2,1,0:T(8,128)S(1)}, f32[4,4,4,2,128,128]{5,4,3,2,1,0:T(8,128)S(1)}, bf16[32,7,128,128]{3,2,1,0:T(8,128)(2,1)S(1)}, s32[4,4,4,2,1,...) custom-call(s32[2,127]{1,0:T(2,128)} %bitcast.33, s32[1]{0:T(128)S(6)} %copy.10.count_ref, ...), custom_call_target="tpu_custom_call" | custom-call | tf_op jit(solution)/shard_map/exchange/pallas_call | solution.py:573
  110.3 9.1 %tiles.1 = f32[1024,32,128]{2,1,0:T(8,128)S(1)} custom-call(s32[1]{0:T(128)S(6)} %copy.10.count_ref, bf16[32,7,128,128]{3,2,1,0:T(8,128)(2,1)S(1)} %get-tuple-element.11.left_ref, f32[32,64,128]{2,1,0:T(8,128)S(1)} %get-tuple-element.12.own_ref, f32[256,64,128]{2,1,0:T(8,128)S(1)} %bitcast.26, s32[128,1,128]{2,1,0:T(1,128)S(1)} %bitcast.27, ...), custom_call_target="tpu_custom_call" | custom-call | tf_op jit(solution)/shard_map/tiles/pallas_call | solution.py:604
  119.4 45.8 %reduce_scatter.1 = f32[256,128]{1,0:T(8,128)S(1)} custom-call(f32[4,4,4,2,256,128]{5,4,3,2,1,0:T(8,128)S(1)} %bitcast.25), custom_call_target="tpu_custom_call" | custom-call | tf_op jit(solution)/shard_map/reduce_scatter/pallas_call | solution.py:548
  165.2 0.2 reshape.34
  165.4 0.8 reshape.35
  (1 shorter events, 0.0 us)

commit v9 on v8

--- a/solution.py
+++ b/solution.py
@@ -347,13 +347,13 @@
 
     count = jnp.minimum(count_ref[0], R)
 
-    def eight(n, carry):
-        for m in range(8):
-            step(8 * n + m, carry)
+    def sixteen(n, carry):
+        for m in range(16):
+            step(16 * n + m, carry)
         return carry
 
-    lax.fori_loop(0, lax.div(count, 8), eight, 0)
-    lax.fori_loop(lax.div(count, 8) * 8, count, step, 0)
+    lax.fori_loop(0, lax.div(count, 16), sixteen, 0)
+    lax.fori_loop(lax.div(count, 16) * 16, count, step, 0)
 
 
 def ring_shapes():

time: 166 us -> 167 us (level)
    pallas_call x1, Pallas kernels: 9.07 us -> 6.21 us  [body(): pl.pallas_call(tile_kernel, grid_spec=pltpu.PrefetchScalarGridSpec(num_sc...]
    pallas_call x1, Pallas kernels: 45.8 us -> 48.5 us  [reduce_scatter(): pl.pallas_call(reduce_kernel, out_shape=jax.ShapeDtypeStruct((OWNER_ROWS,...]
where the time goes in v9:
time: 167 us; the launch traced here: 166 us
  Pallas kernels  164 us (98%)
    pallas_call x1, Pallas kernels, body(): pl.pallas_call(exchange_kernel, in_specs=[smem, smem, vmem, vmem] + [pl.B...  110 us
    pallas_call x1, Pallas kernels, reduce_scatter(): pl.pallas_call(reduce_kernel, out_shape=jax.ShapeDtypeStruct((OWNER_ROWS,...  48.5 us
    pallas_call x1, Pallas kernels, body(): pl.pallas_call(tile_kernel, grid_spec=pltpu.PrefetchScalarGridSpec(num_sc...  6.21 us

profile of v9, /device:TPU:1, one launch (start us, length us, event | category | flops | bytes accessed | tf_op | source)
XLA Modules:
  0.0 166.1 jit_solution(11389529652152617343)
XLA Ops:
  0.7 109.6 %exchange.1 = (f32[32,64,128]{2,1,0:T(8,128)S(1)}, f32[4,4,4,2,128,128]{5,4,3,2,1,0:T(8,128)S(1)}, bf16[32,7,128,128]{3,2,1,0:T(8,128)(2,1)S(1)}, s32[4,4,4,2,1,...) custom-call(s32[2,127]{1,0:T(2,128)} %bitcast.33, s32[1]{0:T(128)S(6)} %copy.10.count_ref, ...), custom_call_target="tpu_custom_call" | custom-call | tf_op jit(solution)/shard_map/exchange/pallas_call | solution.py:573
  110.3 6.2 %tiles.1 = f32[1024,32,128]{2,1,0:T(8,128)S(1)} custom-call(s32[1]{0:T(128)S(6)} %copy.10.count_ref, bf16[32,7,128,128]{3,2,1,0:T(8,128)(2,1)S(1)} %get-tuple-element.11.left_ref, f32[32,64,128]{2,1,0:T(8,128)S(1)} %get-tuple-element.12.own_ref, f32[256,64,128]{2,1,0:T(8,128)S(1)} %bitcast.26, s32[128,1,128]{2,1,0:T(1,128)S(1)} %bitcast.27, ...), custom_call_target="tpu_custom_call" | custom-call | tf_op jit(solution)/shard_map/tiles/pallas_call | solution.py:604
  116.5 48.5 %reduce_scatter.1 = f32[256,128]{1,0:T(8,128)S(1)} custom-call(f32[4,4,4,2,256,128]{5,4,3,2,1,0:T(8,128)S(1)} %bitcast.25), custom_call_target="tpu_custom_call" | custom-call | tf_op jit(solution)/shard_map/reduce_scatter/pallas_call | solution.py:548
  165.1 0.2 reshape.34
  165.3 0.8 reshape.35
  (1 shorter events, 0.0 us)
